TPU v7x, 256 devices: a whole 4x4x8 slice. The times are simulated.
256 devices in a mesh: row: 16 (over y, z_hi, core), col: 16 (over x, z_lo).
Axes of the slice: x: 4, y: 4, z: 8 (z_hi: 2, z_lo: 4; z = z_hi * 4 + z_lo), core: 2. Of those that a mesh axis runs over, the one named last changes fastest.
Arguments:
- inputs: bfloat16 [512, 8192], P(None, 'row'), may hold values from -6 to 6
- out_grad: bfloat16 [512, 8192], P(None, 'row'), may hold values from -6 to 6
- gate_weight: bfloat16 [8192, 28672], P('row', 'col'), may hold values from -0.125 to 0.125
- up_weight: bfloat16 [8192, 28672], P('row', 'col'), may hold values from -0.125 to 0.125
- down_weight: bfloat16 [28672, 8192], P('col', 'row'), may hold values from -0.0625 to 0.0625
- gate_mask: int32 [64, 224], P('row', 'col'), may hold values from 0 to 1, as said below
- up_mask: int32 [64, 224], P('row', 'col'), may hold values from 0 to 1, as said below
- down_mask: int32 [224, 64], P('col', 'row'), may hold values from 0 to 1, as said below
Outputs:
- input_grad: bfloat16 [512, 8192], P('col', 'row')
- gate_grad: bfloat16 [8192, 28672], P('row', 'col')
- up_grad: bfloat16 [8192, 28672], P('row', 'col')
- down_grad: bfloat16 [28672, 8192], P('col', 'row')
Inputs may be any that keep to these rules, and one draw needn't show every extreme that they name: `gate_mask`: 1 marks a kept 128 x 128 block of the gate projection; the share kept varies over row and column blocks. `up_mask`: 1 marks a kept 128 x 128 block of the up projection; the share kept varies over row and column blocks. `down_mask`: 1 marks a kept 128 x 128 block of the down projection; the share kept varies over row and column blocks.
All inputs are finite; a program needn't handle non-finite values.
Results may differ from a plain program's by a relative error of at most 0.0049.
Values may be sent and summed in bfloat16 or wider, within the bound.
A program may use at most 128 MiB of HBM per device.

v0:
```python
import jax
import jax.numpy as jnp
from jax import lax
from jax.sharding import PartitionSpec as P


def spread(values, keep_mask):
    row_blocks, col_blocks = keep_mask.shape
    row_size = values.shape[0] // row_blocks
    col_size = values.shape[1] // col_blocks
    shaped = values.reshape(row_blocks, row_size, col_blocks, col_size)
    return (shaped * keep_mask.astype(values.dtype)[:, None, :, None]).reshape(values.shape)


def contract(former, latter, former_dim, latter_dim):
    return lax.dot_general(
        former,
        latter,
        (((former_dim,), (latter_dim,)), ((), ())),
        preferred_element_type=jnp.float32,
    )


def local_grads(gate_sum, up_sum, back_sum):
    sigmoid_gate = jax.nn.sigmoid(gate_sum)
    hidden = (gate_sum * sigmoid_gate * up_sum).astype(jnp.bfloat16)
    slope = sigmoid_gate * (1.0 + gate_sum * (1.0 - sigmoid_gate))
    gate_delta = (back_sum * up_sum * slope).astype(jnp.bfloat16)
    up_delta = (back_sum * gate_sum * sigmoid_gate).astype(jnp.bfloat16)
    return (hidden, gate_delta, up_delta)


def shards(inputs, out_grad, gate_weight, up_weight, down_weight, gate_mask, up_mask, down_mask):
    gate_full = spread(gate_weight, gate_mask)
    up_full = spread(up_weight, up_mask)
    down_full = spread(down_weight, down_mask)
    rows_in = inputs
    rows_grad = out_grad
    summed = lax.psum_scatter(
        jnp.stack(
            [
                contract(rows_in, gate_full, 1, 0),
                contract(rows_in, up_full, 1, 0),
                contract(rows_grad, down_full, 1, 1),
            ],
            axis=1,
        ),
        "row",
        scatter_dimension=0,
        tiled=True,
    )
    hidden, gate_delta, up_delta = local_grads(summed[:, 0], summed[:, 1], summed[:, 2])
    piece_hidden = lax.all_gather(hidden, "row", axis=0, tiled=True)
    piece_gate = lax.all_gather(gate_delta, "row", axis=0, tiled=True)
    piece_up = lax.all_gather(up_delta, "row", axis=0, tiled=True)
    rows_in = inputs
    rows_grad = out_grad
    grad_gate = contract(rows_in, piece_gate, 0, 0)
    grad_up = contract(rows_in, piece_up, 0, 0)
    grad_down = contract(piece_hidden, rows_grad, 0, 0)
    product = contract(piece_gate, gate_full, 1, 1) + contract(piece_up, up_full, 1, 1)
    partial_value = product
    grad_gate, grad_up, grad_down, partial_value = (grad_gate, grad_up, grad_down, partial_value)
    input_grad = lax.psum_scatter(partial_value, "col", scatter_dimension=0, tiled=True).astype(
        jnp.bfloat16
    )
    gate_grad = spread(grad_gate, gate_mask).astype(jnp.bfloat16)
    up_grad = spread(grad_up, up_mask).astype(jnp.bfloat16)
    down_grad = spread(grad_down, down_mask).astype(jnp.bfloat16)
    return (input_grad, gate_grad, up_grad, down_grad)


def solution(mesh):
    placed = (
        P(None, "row"),
        P(None, "row"),
        P("row", "col"),
        P("row", "col"),
        P("col", "row"),
        P("row", "col"),
        P("row", "col"),
        P("col", "row"),
    )
    return jax.shard_map(
        shards,
        mesh=mesh,
        in_specs=placed,
        out_specs=(P("col", "row"), P("row", "col"), P("row", "col"), P("col", "row")),
        check_vma=False,
    )
```

profile of v0, /device:TPU:32, one launch (start us, length us, event | category | flops | bytes accessed | tf_op | source)
XLA Modules:
  0.0 942.2 jit_solution(6359765616096158785)
XLA Ops:
  7.2 0.8 fusion.17
  8.0 0.1 copy.30
  8.1 4.0 copy.31
  12.1 0.1 copy.28
  12.2 2.3 copy.29
  14.5 0.1 copy.32
  14.6 0.6 mul.93
  15.2 0.8 copy-done.2
  16.0 1.2 convolution_bitcast_fusion.1
  17.2 0.5 mul.90
  17.7 0.9 copy-done.5
  18.7 1.2 convolution_bitcast_fusion.2
  19.9 0.5 mul.96
  20.4 0.6 copy-done.10
  21.0 1.2 convolution_bitcast_fusion
  22.1 5.4 pad_maximum_fusion
  27.5 15.6 %copy.33 = f32[512,3,1792]{2,1,0:T(4,128)} copy(f32[512,3,1792]{0,2,1:T(8,128)} %pad_maximum_fusion) | data formatting | bytes 22020096 | tf_op jit(solution)/shard_map/stack | solution.py:40
  43.2 0.0 all-gather.4.cloned.1.call-start
  43.2 0.6 copy-done.14
  43.8 0.6 dynamic-slice
  45.1 628.2 %all-reduce.3.cloned.1.call-done = f32[512,3,1792]{2,1,0:T(4,128)} async-done(((f32[512,3,1792]{2,1,0:T(4,128)}), f32[512,3,1792]{2,1,0:T(4,128)}) %all-reduce.3.cloned.1.call-update) | async-done | bytes 11010064
  673.3 2.6 constant_dynamic-slice_fusion.2
  675.9 0.9 fusion.15
  676.8 0.0 all-gather.6.cloned.1.call-start
  676.8 0.7 all-gather.6.cloned.1.call-update
  677.6 0.5 all-gather.8.cloned.1.call-update
  678.1 0.2 reduce-scatter.2.cloned.1.call-start
  678.3 56.4 %all-gather.4.cloned.1.call-done = bf16[512,1792]{1,0:T(8,128)(2,1)} async-done(((bf16[32,1792]{1,0:T(8,128)(2,1)}), bf16[512,1792]{1,0:T(8,128)(2,1)}) %all-gather.4.cloned.1.call-update) | async-done | bytes 1835024 | tf_op jit(solution)/shard_map/all_gather | solution.py:54
  734.7 4.7 fusion.4
  739.4 54.7 %all-gather.6.cloned.1.call-done = bf16[512,1792]{1,0:T(8,128)(2,1)} async-done(((bf16[32,1792]{1,0:T(8,128)(2,1)}), bf16[512,1792]{1,0:T(8,128)(2,1)}) %all-gather.6.cloned.1.call-update) | async-done | bytes 1835024 | tf_op jit(solution)/shard_map/all_gather | solution.py:55
  794.1 4.4 convolution_add_fusion
  798.6 0.1 copy.36
  798.7 0.1 copy.37
  798.8 0.1 copy.38
  798.9 0.5 mul.105
  799.4 1.0 copy-done.7
  800.4 1.1 fusion.2
  801.6 2.4 copy.39
  804.0 0.5 mul.108
  804.5 1.0 copy-done.8
  805.5 1.2 fusion.1
  806.6 2.4 copy.40
  809.0 44.4 %all-gather.8.cloned.1.call-done = bf16[512,1792]{1,0:T(8,128)(2,1)} async-done(((bf16[32,1792]{1,0:T(8,128)(2,1)}), bf16[512,1792]{1,0:T(8,128)(2,1)}) %all-gather.8.cloned.1.call-update) | async-done | bytes 1835024 | tf_op jit(solution)/shard_map/all_gather | solution.py:53
  853.4 0.5 mul.113
  854.0 1.0 copy-done.9
  854.9 2.4 fusion
  857.3 76.9 %reduce-scatter.2.cloned.1.call-done = f32[32,512]{1,0:T(8,128)} async-done(((f32[512,512]{1,0:T(8,128)}), f32[32,512]{1,0:T(8,128)}) %reduce-scatter.2.cloned.1.call-update) | async-done | bytes 65552 | tf_op jit(solution)/shard_map/reduce_scatter | solution.py:64
  934.2 1.5 convert_element_type.44
  (30 shorter events, 0.2 us)
Async XLA Ops:
  7.2 8.0 copy-start
  7.2 666.1 %all-reduce.3.cloned.1.call-start = ((), (), s32[]{:S(2)}) async-start(), calls=%async_computation.5 | async-start | bytes 29360128
  8.1 4.0 copy-start.11
  8.1 4.1 copy-start.1
  12.2 2.3 copy-start.12
  14.5 1.5 copy-start.2
  15.2 2.0 copy-start.4
  17.2 1.5 copy-start.5
  17.7 2.1 copy-start.6
  18.7 1.7 copy-start.13
  19.8 1.1 copy-start.10
  43.1 0.7 copy-start.14
  43.2 691.5 %all-gather.4.cloned.1.call-start = ((), (), s32[]{:S(2)}) async-start(), calls=%async_computation.1 | async-start | bytes 1949696 | tf_op jit(solution)/shard_map/all_gather | solution.py:54
  676.8 117.4 %all-gather.6.cloned.1.call-start = ((), (), s32[]{:S(2)}) async-start(), calls=%async_computation.2 | async-start | bytes 1949696 | tf_op jit(solution)/shard_map/all_gather | solution.py:55
  677.5 175.9 %all-gather.8.cloned.1.call-start = ((), (), s32[]{:S(2)}) async-start(), calls=%async_computation.4 | async-start | bytes 1949696 | tf_op jit(solution)/shard_map/all_gather | solution.py:53
  678.1 116.1 %copy-start.3 = (bf16[512,1792]{0,1:T(8,128)(2,1)S(1)}, bf16[512,1792]{0,1:T(8,128)(2,1)}, u32[]{:S(2)}) copy-start(bf16[512,1792]{0,1:T(8,128)(2,1)} %copy.31) | copy-start | bytes 5505028
  678.1 256.1 %reduce-scatter.2.cloned.1.call-start = ((), (), s32[]{:S(2)}) async-start(), calls=%async_computation.3 | async-start | bytes 1114112 | tf_op jit(solution)/shard_map/reduce_scatter | solution.py:64
  798.9 1.5 copy-start.7
  804.0 1.5 copy-start.8
  853.4 1.5 copy-start.9
Sparse Core Ops, SparseCore 0:
  43.3 629.9 all-reduce.2
  676.9 57.7 all-gather.3
  737.4 56.6 all-gather.5
  796.7 56.6 all-gather.7
  855.8 78.3 reduce-scatter.1
where the time goes:
time: 948 us; the launch traced here: 942 us
  waiting for transfers between devices  862 us (91%)
  local copies, waits for them, and re-layouts  39.6 us (4%)
  matrix products  17.3 us (2%)
  between operations  14.6 us (2%)
    unnamed x6, waiting for transfers between devices  629 us
    reduce_scatter x1, waiting for transfers between devices, shards(): lax.psum_scatter(partial_value, 'col', scatter_dimension=0, tiled=True)  76.9 us
    all_gather x1, waiting for transfers between devices, shards(): piece_gate = lax.all_gather(gate_delta, 'row', axis=0, tiled=True)  56.4 us
    all_gather x1, waiting for transfers between devices, shards(): piece_up = lax.all_gather(up_delta, 'row', axis=0, tiled=True)  54.7 us
    all_gather x1, waiting for transfers between devices, shards(): piece_hidden = lax.all_gather(hidden, 'row', axis=0, tiled=True)  44.4 us
  transfers between devices with their start and end apart: 5, of which 5 were waited for; matrix products, arithmetic and copies ran while one was open for 2% of the time, Pallas kernels for 0%

commit v1 on v0

v1 whole, which is shorter than its diff:
```python
import jax
import jax.numpy as jnp
from jax import lax
from jax.experimental import pallas as pl
from jax.experimental.pallas import tpu as pltpu
from jax.sharding import PartitionSpec as P

MESH = pl.DeviceIdType.MESH
F32 = jnp.float32
BF16 = jnp.bfloat16
BLOCK = 128
TOK = 512
DIM = 512
FF = 1792
HALF = FF // 2
CHUNKS = 4
ROWS = 16
STEPS = 3 * CHUNKS

LAG_FORWARD = 2
LAG_OWN = 4
LAG_FINAL = 7
LAG_SPREAD = 10
LAG_RELAY = 12
LAG_CORE = 14
LAG_GRAD = 15

R1, R2, R3, L1, L2, L3 = range(6)


def product(left, right):
    return jnp.dot(left, right, preferred_element_type=F32)


def product_t(left, right):
    return lax.dot_general(left, right, (((1,), (1,)), ((), ())), preferred_element_type=F32)


def t_product(left, right):
    return lax.dot_general(left, right, (((0,), (0,)), ((), ())), preferred_element_type=F32)


def exchange_kernel(
    x_hbm, og_hbm, wg_hbm, wu_hbm, wd_hbm, gm, um, dm,
    d_hbm, ig_out,
    x_own, og_own, x_oth, og_oth, w_own, wd_own, w_oth, wd_oth,
    part, send, ring, z_out, z_in, halves, final, deltas,
    ig, ig_send, ig_ring, ig_sum, ig_in,
    local_sem, core_s, core_r, ring_s, ring_r, z_s, z_r, ag_s, ag_r, x_s, x_r, zl_s, zl_r,
):
    row = lax.axis_index("row")
    col = lax.axis_index("col")
    y = row // 4
    h = (row // 2) % 2
    c = row % 2
    x = col // 4
    zl = col % 4
    up = lax.rem(y + 1, 4)
    down = lax.rem(y + 3, 4)
    far = lax.rem(y + 2, 4)
    right = (up * 4 + h * 2 + c, col)
    left = (down * 4 + h * 2 + c, col)
    z_dev = (y * 4 + (1 - h) * 2 + c, col)
    core_dev = (y * 4 + h * 2 + (1 - c), col)
    x_right = (row, lax.rem(x + 1, 4) * 4 + zl)
    x_left = (row, lax.rem(x + 3, 4) * 4 + zl)
    own_cols = pl.ds(pl.multiple_of(c * HALF, 128), HALF)
    oth_cols = pl.ds(pl.multiple_of((1 - c) * HALF, 128), HALF)

    def remote(src, dst, ss, rs, dev):
        return pltpu.make_async_remote_copy(
            src_ref=src, dst_ref=dst, send_sem=ss, recv_sem=rs, device_id=dev, device_id_type=MESH
        )

    def piece(yy, hh):
        return pl.ds(pl.multiple_of(yy * 32 + hh * ROWS, ROWS), ROWS)

    loads = [
        pltpu.make_async_copy(wg_hbm, w_own.at[0], local_sem.at[0]),
        pltpu.make_async_copy(x_hbm, x_own, local_sem.at[1]),
        pltpu.make_async_copy(wu_hbm, w_own.at[1], local_sem.at[2]),
        pltpu.make_async_copy(wd_hbm, wd_own, local_sem.at[3]),
        pltpu.make_async_copy(og_hbm, og_own, local_sem.at[4]),
    ]
    for load in loads:
        load.start()

    bar = pltpu.get_barrier_semaphore()
    friends = [right, left, z_dev, core_dev, x_right, x_left]
    friends += [(row, x * 4 + lax.rem(zl + d, 4)) for d in (1, 2, 3)]
    for dev in friends:
        pl.semaphore_signal(bar, inc=1, device_id=dev, device_id_type=MESH)
    pl.semaphore_wait(bar, len(friends))

    core_sends = [
        remote(x_hbm, x_oth, core_s.at[0], core_r.at[0], core_dev),
        remote(w_own.at[0, :, oth_cols], w_oth.at[0], core_s.at[1], core_r.at[1], core_dev),
        remote(w_own.at[1, :, oth_cols], w_oth.at[1], core_s.at[2], core_r.at[2], core_dev),
        remote(og_hbm, og_oth, core_s.at[3], core_r.at[3], core_dev),
        remote(wd_own.at[pl.ds(pl.multiple_of((1 - c) * HALF, 128), HALF)], wd_oth, core_s.at[4], core_r.at[4], core_dev),
    ]
    core_sends[0].start()

    def mask_cols(which, mask_ref):
        @pl.loop(0, FF // BLOCK)
        def _(j):
            cols = pl.ds(pl.multiple_of(j * BLOCK, BLOCK), BLOCK)
            for i in range(DIM // BLOCK):
                rows = pl.ds(i * BLOCK, BLOCK)
                keep = jnp.full((BLOCK, BLOCK), mask_ref[i, j].astype(F32), F32).astype(BF16)
                w_own[which, rows, cols] = w_own[which, rows, cols] * keep

    def mask_rows():
        @pl.loop(0, FF // BLOCK)
        def _(j):
            rows = pl.ds(pl.multiple_of(j * BLOCK, BLOCK), BLOCK)
            for i in range(DIM // BLOCK):
                cols = pl.ds(i * BLOCK, BLOCK)
                keep = jnp.full((BLOCK, BLOCK), dm[j, i].astype(F32), F32).astype(BF16)
                wd_own[rows, cols] = wd_own[rows, cols] * keep

    loads[0].wait()
    mask_cols(0, gm)
    core_sends[1].start()
    loads[2].wait()
    mask_cols(1, um)
    core_sends[2].start()
    core_sends[3].start()
    loads[3].wait()
    mask_rows()
    core_sends[4].start()
    loads[1].wait()
    loads[4].wait()

    def ring_copy(kind, s, yy, hh):
        dev = right if kind in (R1, R2, R3) else left
        return remote(send.at[s, piece(yy, hh)], ring.at[kind, s], ring_s.at[kind, s], ring_r.at[kind, s], dev)

    def ring_pieces(s):
        return [
            ring_copy(R1, s, far, 0),
            ring_copy(L1, s, far, 1),
            ring_copy(R2, s, up, 1),
            ring_copy(L2, s, down, 0),
            ring_copy(R3, s, up, 0),
            ring_copy(L3, s, down, 1),
        ]

    def z_copy(s):
        return remote(z_out.at[s], z_in.at[s], z_s.at[s], z_r.at[s], z_dev)

    def ag_copy(t, k, yy, hh, dev):
        ref = deltas.at[pl.ds(1, 2), t, piece(yy, hh), own_cols]
        return remote(ref, ref, ag_s.at[t, k], ag_r.at[t, k], dev)

    def ag_core(t):
        ref = deltas.at[pl.ds(1, 2), t, :, own_cols]
        return remote(ref, ref, ag_s.at[t, 7], ag_r.at[t, 7], core_dev)

    def ag_core_in(t):
        ref = deltas.at[pl.ds(1, 2), t, :, oth_cols]
        return remote(ref, ref, ag_s.at[t, 7], ag_r.at[t, 7], core_dev)

    def h_copy(k, yy, hh, dev):
        ref = deltas.at[0, :, piece(yy, hh), own_cols]
        return remote(ref, ref, ag_s.at[CHUNKS, k], ag_r.at[CHUNKS, k], dev)

    def gather_own(copy):
        copy(0, y, h, z_dev).start()
        copy(1 + h, y, h, right).start()
        copy(3 + h, y, h, left).start()

    def gather_partner(copy):
        copy(0, y, 1 - h, z_dev).wait_recv()
        copy(2 - h, y, 1 - h, right).start()
        copy(4 - h, y, 1 - h, left).start()

    def gather_relay(copy):
        copy(1, down, 0, right).wait_recv()
        copy(5, down, 0, right).start()
        copy(4, up, 1, left).wait_recv()
        copy(6, up, 1, left).start()

    def gather_rest(copy):
        copy(2, down, 1, right).wait_recv()
        copy(3, up, 0, left).wait_recv()
        copy(5, far, 0, right).wait_recv()
        copy(6, far, 1, left).wait_recv()

    def gather_drain(copy):
        copy(0, y, h, z_dev).wait_send()
        for hh in range(2):
            copy(1 + hh, y, hh, right).wait_send()
            copy(3 + hh, y, hh, left).wait_send()
        copy(5, down, 0, right).wait_send()
        copy(6, up, 1, left).wait_send()

    def out_copy(t):
        return pltpu.make_async_copy(deltas.at[pl.ds(1, 2), t], d_hbm.at[pl.ds(1, 2), t], local_sem.at[5 + t])

    def at_chunk(s, lag, fn):
        @pl.when((s >= lag + 2) & (s < STEPS + lag) & (lax.rem(s + 3 * 16 - lag, 3) == 2))
        def _():
            fn((s - lag) // 3)

    @pl.loop(0, STEPS + LAG_GRAD)
    def _(s):
        @pl.when(s < STEPS)
        def _():
            m = lax.rem(s, 3)
            t = s // 3
            rows = pl.ds(pl.multiple_of(t * 128, 128), 128)

            @pl.when(s == 0)
            def _():
                core_sends[0].wait_recv()
                core_sends[1].wait_recv()

            @pl.when(s == 1)
            def _():
                core_sends[2].wait_recv()

            @pl.when(s == 2)
            def _():
                core_sends[3].wait_recv()
                core_sends[4].wait_recv()

            @pl.when(m < 2)
            def _():
                p = product(x_own[rows, :], w_own[m, :, own_cols]) + product(x_oth[rows, :], w_oth[m])
                part[s] = p
                send[s] = p.astype(BF16)

            @pl.when(m == 2)
            def _():
                mine = wd_own[own_cols, :]
                p = product_t(og_own[rows, :], mine) + product_t(og_oth[rows, :], wd_oth[...])
                part[s] = p
                send[s] = p.astype(BF16)

            for copy in ring_pieces(s)[:4]:
                copy.start()

        @pl.when((s >= LAG_FORWARD) & (s < STEPS + LAG_FORWARD))
        def _():
            n = s - LAG_FORWARD
            copies = ring_pieces(n)
            copies[0].wait_recv()
            send[n, piece(up, 0)] = (part[n, piece(up, 0)] + ring[R1, n].astype(F32)).astype(BF16)
            copies[4].start()
            copies[1].wait_recv()
            send[n, piece(down, 1)] = (part[n, piece(down, 1)] + ring[L1, n].astype(F32)).astype(BF16)
            copies[5].start()

        @pl.when((s >= LAG_OWN) & (s < STEPS + LAG_OWN))
        def _():
            n = s - LAG_OWN
            copies = ring_pieces(n)
            for copy in copies[2:]:
                copy.wait_recv()
            halves[n, 0] = part[n, piece(y, 0)] + ring[R3, n].astype(F32) + ring[L2, n].astype(F32)
            halves[n, 1] = part[n, piece(y, 1)] + ring[L3, n].astype(F32) + ring[R2, n].astype(F32)
            z_out[n] = halves[n, 1 - h].astype(BF16)
            z_copy(n).start()

        @pl.when((s >= LAG_FINAL) & (s < STEPS + LAG_FINAL))
        def _():
            n = s - LAG_FINAL
            z_copy(n).wait_recv()
            final[n] = halves[n, h] + z_in[n].astype(F32)

        def pointwise(t):
            gate = final[3 * t]
            upv = final[3 * t + 1]
            back = final[3 * t + 2]
            sig = jax.nn.sigmoid(gate)
            mine = piece(y, h)
            deltas[0, t, mine, own_cols] = (gate * sig * upv).astype(BF16)
            slope = sig * (1.0 + gate * (1.0 - sig))
            deltas[1, t, mine, own_cols] = (back * upv * slope).astype(BF16)
            deltas[2, t, mine, own_cols] = (back * gate * sig).astype(BF16)
            gather_own(lambda *a: ag_copy(t, *a))

            @pl.when(t == CHUNKS - 1)
            def _():
                h_copy(0, y, h, z_dev).start()

        def spread_partner(t):
            gather_partner(lambda *a: ag_copy(t, *a))

            @pl.when(t == CHUNKS - 1)
            def _():
                h_copy(1 + h, y, h, right).start()
                h_copy(3 + h, y, h, left).start()

        def relay(t):
            gather_relay(lambda *a: ag_copy(t, *a))

            @pl.when(t == CHUNKS - 1)
            def _():
                gather_partner(h_copy)

        def to_core(t):
            gather_rest(lambda *a: ag_copy(t, *a))
            ag_core(t).start()

        def grad(t):
            ag_core_in(t).wait_recv()
            out_copy(t).start()
            value = product_t(deltas[1, t], w_own[0]) + product_t(deltas[2, t], w_own[1])
            ig[t] = value
            ig_send[t] = value.astype(BF16)

        at_chunk(s, LAG_FINAL, pointwise)
        at_chunk(s, LAG_SPREAD, spread_partner)
        at_chunk(s, LAG_RELAY, relay)
        at_chunk(s, LAG_CORE, to_core)
        at_chunk(s, LAG_GRAD, grad)

    x_up = lax.rem(x + 1, 4)
    x_down = lax.rem(x + 3, 4)
    x_far = lax.rem(x + 2, 4)

    def x_copy(kind, q, half):
        dev = x_right if kind in (R1, R2, R3) else x_left
        return remote(ig_send.at[q, pl.ds(half * 64, 64)], ig_ring.at[kind], x_s.at[kind], x_r.at[kind], dev)

    x_copies = [
        x_copy(R1, x_far, 0),
        x_copy(L1, x_far, 1),
        x_copy(R2, x_up, 1),
        x_copy(L2, x_down, 0),
        x_copy(R3, x_up, 0),
        x_copy(L3, x_down, 1),
    ]
    for copy in x_copies[:4]:
        copy.start()
    gather_relay(h_copy)
    x_copies[0].wait_recv()
    ig_send[x_up, pl.ds(0, 64)] = (ig[x_up, pl.ds(0, 64)] + ig_ring[R1].astype(F32)).astype(BF16)
    x_copies[4].start()
    x_copies[1].wait_recv()
    ig_send[x_down, pl.ds(64, 64)] = (ig[x_down, pl.ds(64, 64)] + ig_ring[L1].astype(F32)).astype(BF16)
    x_copies[5].start()
    for copy in x_copies[2:]:
        copy.wait_recv()
    ig_sum[pl.ds(0, 64)] = ig[x, pl.ds(0, 64)] + ig_ring[R3].astype(F32) + ig_ring[L2].astype(F32)
    ig_sum[pl.ds(64, 64)] = ig[x, pl.ds(64, 64)] + ig_ring[L3].astype(F32) + ig_ring[R2].astype(F32)

    def zl_copy(d):
        to = lax.rem(zl + d, 4)
        return remote(
            ig_sum.at[pl.ds(pl.multiple_of(to * 32, 32), 32)], ig_in.at[d - 1], zl_s.at[d - 1], zl_r.at[d - 1], (row, x * 4 + to)
        )

    for d in (2, 3, 1):
        zl_copy(d).start()

    gather_rest(h_copy)
    h_ref = deltas.at[0, :, :, own_cols]
    h_core = remote(h_ref, h_ref, ag_s.at[CHUNKS, 7], ag_r.at[CHUNKS, 7], core_dev)
    h_core.start()

    total = ig_sum[pl.ds(pl.multiple_of(zl * 32, 32), 32)]
    for d in (1, 2, 3):
        zl_copy(d).wait_recv()
        total = total + ig_in[d - 1]
    ig_out[...] = total.astype(BF16)

    h_in = deltas.at[0, :, :, oth_cols]
    remote(h_in, h_in, ag_s.at[CHUNKS, 7], ag_r.at[CHUNKS, 7], core_dev).wait_recv()
    h_store = pltpu.make_async_copy(deltas.at[0], d_hbm.at[0], local_sem.at[5 + CHUNKS])
    h_store.start()

    for copy in core_sends:
        copy.wait_send()

    @pl.loop(0, STEPS)
    def _(s):
        for copy in ring_pieces(s):
            copy.wait_send()
        z_copy(s).wait_send()

    @pl.loop(0, CHUNKS)
    def _(t):
        gather_drain(lambda *a: ag_copy(t, *a))
        ag_core(t).wait_send()
        out_copy(t).wait()

    gather_drain(h_copy)
    h_core.wait_send()
    for copy in x_copies:
        copy.wait_send()
    for d in (1, 2, 3):
        zl_copy(d).wait_send()
    h_store.wait()


def exchange(inputs, out_grad, gate_weight, up_weight, down_weight, gate_mask, up_mask, down_mask):
    any_spec = pl.BlockSpec(memory_space=pl.ANY)
    smem = pl.BlockSpec(memory_space=pltpu.SMEM)
    dma = pltpu.SemaphoreType.DMA
    return pl.pallas_call(
        exchange_kernel,
        out_shape=(
            jax.ShapeDtypeStruct((3, CHUNKS, 128, FF), BF16),
            jax.ShapeDtypeStruct((32, DIM), BF16),
        ),
        in_specs=[any_spec] * 5 + [smem] * 3,
        out_specs=(any_spec, pl.BlockSpec(memory_space=pltpu.VMEM)),
        scratch_shapes=[
            pltpu.VMEM((TOK, DIM), BF16),
            pltpu.VMEM((TOK, DIM), BF16),
            pltpu.VMEM((TOK, DIM), BF16),
            pltpu.VMEM((TOK, DIM), BF16),
            pltpu.VMEM((2, DIM, FF), BF16),
            pltpu.VMEM((FF, DIM), BF16),
            pltpu.VMEM((2, DIM, HALF), BF16),
            pltpu.VMEM((HALF, DIM), BF16),
            pltpu.VMEM((STEPS, 128, HALF), F32),
            pltpu.VMEM((STEPS, 128, HALF), BF16),
            pltpu.VMEM((6, STEPS, ROWS, HALF), BF16),
            pltpu.VMEM((STEPS, ROWS, HALF), BF16),
            pltpu.VMEM((STEPS, ROWS, HALF), BF16),
            pltpu.VMEM((STEPS, 2, ROWS, HALF), F32),
            pltpu.VMEM((STEPS, ROWS, HALF), F32),
            pltpu.VMEM((3, CHUNKS, 128, FF), BF16),
            pltpu.VMEM((CHUNKS, 128, DIM), F32),
            pltpu.VMEM((CHUNKS, 128, DIM), BF16),
            pltpu.VMEM((6, 64, DIM), BF16),
            pltpu.VMEM((128, DIM), F32),
            pltpu.VMEM((3, 32, DIM), F32),
            dma((6 + CHUNKS,)),
            dma((5,)),
            dma((5,)),
            dma((6, STEPS)),
            dma((6, STEPS)),
            dma((STEPS,)),
            dma((STEPS,)),
            dma((CHUNKS + 1, 8)),
            dma((CHUNKS + 1, 8)),
            dma((6,)),
            dma((6,)),
            dma((3,)),
            dma((3,)),
        ],
        compiler_params=pltpu.CompilerParams(
            collective_id=0, has_side_effects=True, vmem_limit_bytes=56 * 2**20
        ),
        name="exchange",
    )(inputs, out_grad, gate_weight, up_weight, down_weight, gate_mask, up_mask, down_mask)


def grads_kernel(x_ref, og_ref, d_ref, gm, um, dm, ig_ref, gate_out, up_out, down_out, ig_out):
    j = pl.program_id(0)
    ig_out[...] = ig_ref[...]
    for which, mask, out in ((1, gm, gate_out), (2, um, up_out)):
        value = t_product(x_ref[...], d_ref[which])
        for i in range(DIM // BLOCK):
            for k in range(2):
                keep = mask[i, 2 * j + k].astype(F32)
                blk = (slice(i * BLOCK, (i + 1) * BLOCK), slice(k * BLOCK, (k + 1) * BLOCK))
                out[blk] = (value[blk] * keep).astype(BF16)
    value = t_product(d_ref[0], og_ref[...])
    for k in range(2):
        for i in range(DIM // BLOCK):
            keep = dm[2 * j + k, i].astype(F32)
            blk = (slice(k * BLOCK, (k + 1) * BLOCK), slice(i * BLOCK, (i + 1) * BLOCK))
            down_out[blk] = (value[blk] * keep).astype(BF16)


def grads(inputs, out_grad, deltas, gate_mask, up_mask, down_mask, ig):
    smem = pl.BlockSpec(memory_space=pltpu.SMEM)
    whole = pl.BlockSpec((TOK, DIM), lambda j: (0, 0))
    ig_spec = pl.BlockSpec((32, DIM), lambda j: (0, 0))
    return pl.pallas_call(
        grads_kernel,
        grid=(FF // 256,),
        out_shape=(
            jax.ShapeDtypeStruct((DIM, FF), BF16),
            jax.ShapeDtypeStruct((DIM, FF), BF16),
            jax.ShapeDtypeStruct((FF, DIM), BF16),
            jax.ShapeDtypeStruct((32, DIM), BF16),
        ),
        in_specs=[whole, whole, pl.BlockSpec((3, TOK, 256), lambda j: (0, 0, j)), smem, smem, smem, ig_spec],
        out_specs=(
            pl.BlockSpec((DIM, 256), lambda j: (0, j)),
            pl.BlockSpec((DIM, 256), lambda j: (0, j)),
            pl.BlockSpec((256, DIM), lambda j: (j, 0)),
            ig_spec,
        ),
        name="grads",
    )(inputs, out_grad, deltas, gate_mask, up_mask, down_mask, ig)


def shards(inputs, out_grad, gate_weight, up_weight, down_weight, gate_mask, up_mask, down_mask):
    deltas, ig = exchange(inputs, out_grad, gate_weight, up_weight, down_weight, gate_mask, up_mask, down_mask)
    deltas = deltas.reshape(3, TOK, FF)
    gate_grad, up_grad, down_grad, input_grad = grads(inputs, out_grad, deltas, gate_mask, up_mask, down_mask, ig)
    return (input_grad, gate_grad, up_grad, down_grad)


def solution(mesh):
    placed = (
        P(None, "row"),
        P(None, "row"),
        P("row", "col"),
        P("row", "col"),
        P("col", "row"),
        P("row", "col"),
        P("row", "col"),
        P("col", "row"),
    )
    return jax.shard_map(
        shards,
        mesh=mesh,
        in_specs=placed,
        out_specs=(P("col", "row"), P("row", "col"), P("row", "col"), P("col", "row")),
        check_vma=False,
    )
```

time: 948 us -> 99 us (0.10)
  the two profiles are of different devices: /device:TPU:32 before, /device:TPU:1 now
where the time goes in v1:
time: 99 us; the launch traced here: 98.7 us
  Pallas kernels  96.7 us (98%)
  local copies, waits for them, and re-layouts  1.36 us (1%)
    pallas_call x1, Pallas kernels, exchange(): pl.pallas_call(exchange_kernel, out_shape=(jax.ShapeDtypeStruct((3, CHUNK...  88 us
    pallas_call x1, Pallas kernels, grads(): pl.pallas_call(grads_kernel, grid=(FF // 256,), out_shape=(jax.ShapeDtype...  8.68 us

profile of v1, /device:TPU:1, one launch (start us, length us, event | category | flops | bytes accessed | tf_op | source)
XLA Modules:
  0.0 98.7 jit_solution(10189301075141632298)
XLA Ops:
  0.6 1.4 %copy.12.dm = s32[14,4]{1,0:T(8,128)} copy(s32[14,4]{0,1:T(4,128)} %param.15) | data formatting | bytes 448 | tf_op args[7]
  2.0 88.0 %exchange.1 = (bf16[3,4,128,1792]{3,2,1,0:T(8,128)(2,1)}, bf16[32,512]{1,0:T(8,128)(2,1)}) custom-call(bf16[512,512]{1,0:T(8,128)(2,1)} %x_ref.1, bf16[512,512]{1,0:T(8,128)(2,1)} %og_ref.1, bf16[512,1792]{1,0:T(8,128)(2,1)} %wg_hbm.1, bf16[512,1792]{1,0:T(8,128)(2,1)} %wu_hbm.1, bf16[1792,512]{1,0:T(8,128)(2,1)} %wd_hbm.1, s32[4,14]{1,0:T(4,128)} %gm.3, ...), custom_call_target="tpu_custom_call" | custom-call | tf_op jit(solution)/shard_map/exchange/pallas_call | solution.py:403
  90.0 8.7 %grads.1 = (bf16[512,1792]{1,0:T(8,128)(2,1)}, bf16[512,1792]{1,0:T(8,128)(2,1)}, bf16[1792,512]{1,0:T(8,128)(2,1)}, bf16[32,512]{1,0:T(8,128)(2,1)}) custom-call(bf16[512,512]{1,0:T(8,128)(2,1)} %x_ref.1, bf16[512,512]{1,0:T(8,128)(2,1)} %og_ref.1, bf16[3,512,1792]{2,1,0:T(8,128)(2,1)} %bitcast.1, s32[4,14]{1,0:T(4,128)} %gm.3, s32[4,14]{1,0:T(4,128)} %um.3, ...), custom_call_target="tpu_custom_call" | custom-call | tf_op jit(solution)/shard_map/grads/pallas_call | solution.py:476

commit v2 on v0

v2 whole, which is shorter than its diff:
```python
import jax
import jax.numpy as jnp
from jax import lax
from jax.experimental import pallas as pl
from jax.experimental.pallas import tpu as pltpu
from jax.sharding import PartitionSpec as P

MESH = pl.DeviceIdType.MESH
F32 = jnp.float32
BF16 = jnp.bfloat16
BLOCK = 128
TOK = 512
DIM = 512
FF = 1792
HALF = FF // 2
CHUNKS = 4
ROWS = 16
STEPS = 3 * CHUNKS

LAG_RING = 1
LAG_FORWARD = 3
LAG_OWN = 5
LAG_FINAL = 9
LAG_RELAY = 11
LAG_CORE = 13
LAG_GRAD = 14
LAG_COL = 16
TURN = 13

R1, R2, R3, L1, L2, L3 = range(6)


def product(left, right):
    return jnp.dot(left, right, preferred_element_type=F32)


def product_t(left, right):
    return lax.dot_general(left, right, (((1,), (1,)), ((), ())), preferred_element_type=F32)


def t_product(left, right):
    return lax.dot_general(left, right, (((0,), (0,)), ((), ())), preferred_element_type=F32)


def exchange_kernel(
    x_hbm, og_hbm, wg_hbm, wu_hbm, wd_hbm, gm, um, dm,
    d_hbm, xt_hbm, ig_out,
    x_own, og_own, xt, w_own, wd_own, core_out, core_in,
    part, send, ring, z_out, z_in, sums, deltas,
    ig, ig_x, ig_z, ig_sum, ig_in,
    local_sem, core_s, core_r, ring_s, ring_r, z_s, z_r, ag_s, ag_r, x_s, x_r, zl_s, zl_r,
):
    row = lax.axis_index("row")
    col = lax.axis_index("col")
    y = row // 4
    h = (row // 2) % 2
    c = row % 2
    x = col // 4
    zl = col % 4
    up = lax.rem(y + 1, 4)
    down = lax.rem(y + 3, 4)
    far = lax.rem(y + 2, 4)

    def ring_dev(yy):
        return (yy * 4 + h * 2 + c, col)

    right = ring_dev(up)
    left = ring_dev(down)
    z_dev = (y * 4 + (1 - h) * 2 + c, col)
    core_dev = (y * 4 + h * 2 + (1 - c), col)
    own_cols = pl.ds(pl.multiple_of(c * HALF, 128), HALF)
    oth_cols = pl.ds(pl.multiple_of((1 - c) * HALF, 128), HALF)

    def x_dev(d):
        return (row, lax.rem(x + d, 4) * 4 + zl)

    def remote(src, dst, ss, rs, dev):
        return pltpu.make_async_remote_copy(
            src_ref=src, dst_ref=dst, send_sem=ss, recv_sem=rs, device_id=dev, device_id_type=MESH
        )

    def chunk(k):
        return lax.rem(k + 2, 4)

    def piece(yy, hh):
        return pl.ds(pl.multiple_of(yy * 32 + hh * ROWS, ROWS), ROWS)

    def half(hh):
        return pl.ds(pl.multiple_of(hh * ROWS, ROWS), ROWS)

    loads = [
        pltpu.make_async_copy(x_hbm, x_own, local_sem.at[0]),
        pltpu.make_async_copy(wg_hbm, w_own.at[0], local_sem.at[1]),
        pltpu.make_async_copy(wu_hbm, w_own.at[1], local_sem.at[2]),
        pltpu.make_async_copy(og_hbm, og_own, local_sem.at[3]),
        pltpu.make_async_copy(wd_hbm, wd_own, local_sem.at[4]),
    ]
    for load in loads:
        load.start()

    bar = pltpu.get_barrier_semaphore()
    friends = [right, left, z_dev, core_dev] + [x_dev(d) for d in (1, 2, 3)]
    friends += [(row, x * 4 + lax.rem(zl + d, 4)) for d in (1, 2, 3)]
    for dev in friends:
        pl.semaphore_signal(bar, inc=1, device_id=dev, device_id_type=MESH)
    pl.semaphore_wait(bar, len(friends))

    def mask_cols(which, mask_ref):
        @pl.loop(0, FF // BLOCK)
        def _(j):
            cols = pl.ds(pl.multiple_of(j * BLOCK, BLOCK), BLOCK)
            for i in range(DIM // BLOCK):
                rows = pl.ds(i * BLOCK, BLOCK)
                keep = jnp.full((BLOCK, BLOCK), mask_ref[i, j].astype(F32), F32).astype(BF16)
                w_own[which, rows, cols] = w_own[which, rows, cols] * keep

    def mask_rows():
        @pl.loop(0, FF // BLOCK)
        def _(j):
            rows = pl.ds(pl.multiple_of(j * BLOCK, BLOCK), BLOCK)
            for i in range(DIM // BLOCK):
                cols = pl.ds(i * BLOCK, BLOCK)
                keep = jnp.full((BLOCK, BLOCK), dm[i, j].astype(F32), F32).astype(BF16)
                wd_own[rows, cols] = wd_own[rows, cols] * keep

    def core_copy(s):
        return remote(core_out.at[s], core_in.at[s], core_s.at[s], core_r.at[s], core_dev)

    def ring_copy(kind, s, yy, hh):
        dev = right if kind in (R1, R2, R3) else left
        return remote(send.at[s, piece(yy, hh)], ring.at[kind, s], ring_s.at[kind, s], ring_r.at[kind, s], dev)

    def ring_early(s):
        return [ring_copy(R1, s, far, 0), ring_copy(L1, s, far, 1), ring_copy(R2, s, up, 1), ring_copy(L2, s, down, 0)]

    def ring_late(s):
        return [ring_copy(R3, s, up, 0), ring_copy(L3, s, down, 1)]

    def z_copy(s):
        return remote(z_out.at[s], z_in.at[s], z_s.at[s], z_r.at[s], z_dev)

    def y_copy(m, k):
        def copy(i, yy, hh, dev):
            ref = deltas.at[m, k, yy, half(hh), own_cols]
            return remote(ref, ref, ag_s.at[m, k, i], ag_r.at[m, k, i], dev)

        return copy

    def pair_copy(m, k, cols):
        ref = deltas.at[m, k, :, :, cols]
        return remote(ref, ref, ag_s.at[m, k, 6], ag_r.at[m, k, 6], core_dev)

    def gather_own(copy):
        copy(0, y, 0, right).start()
        copy(3, y, 1, left).start()
        copy(1, y, 1, right).start()
        copy(2, y, 0, left).start()

    def gather_relay(copy):
        copy(0, down, 0, right).wait_recv()
        copy(4, down, 0, right).start()
        copy(3, up, 1, left).wait_recv()
        copy(5, up, 1, left).start()

    def gather_rest(copy):
        copy(1, down, 1, right).wait_recv()
        copy(2, up, 0, left).wait_recv()
        copy(4, far, 0, right).wait_recv()
        copy(5, far, 1, left).wait_recv()

    def gather_drain(copy):
        for hh in range(2):
            copy(hh, y, hh, right).wait_send()
            copy(2 + hh, y, hh, left).wait_send()
        copy(4, down, 0, right).wait_send()
        copy(5, up, 1, left).wait_send()

    def out_copy(k):
        return pltpu.make_async_copy(
            deltas.at[pl.ds(1, 2), k], d_hbm.at[pl.ds(1, 2), :, chunk(k)], local_sem.at[5 + k]
        )

    def hidden_store(k):
        return pltpu.make_async_copy(deltas.at[0, k], d_hbm.at[0, :, chunk(k)], local_sem.at[10 + k])

    xt_copy = pltpu.make_async_copy(xt, xt_hbm, local_sem.at[9])

    def x_copy(k, d):
        return remote(
            ig.at[k, lax.rem(x + d, 4)], ig_x.at[k, d - 1], x_s.at[k, d - 1], x_r.at[k, d - 1], x_dev(d)
        )

    def zl_copy(k):
        slot = lax.rem(zl - chunk(k) + 7, 4)
        return remote(ig_z.at[k], ig_in.at[slot], zl_s.at[k], zl_r.at[slot], (row, x * 4 + chunk(k)))

    def reduce_col(k):
        total = ig[k, x]
        for d in (1, 2, 3):
            x_copy(k, d).wait_recv()
            total = total + ig_x[k, d - 1]

        @pl.when(zl == chunk(k))
        def _():
            ig_sum[...] = total

        @pl.when(zl != chunk(k))
        def _():
            ig_z[k] = total.astype(BF16)
            zl_copy(k).start()

    def at_chunk(s, lag, fn, count=CHUNKS):
        @pl.when((s >= lag + 2) & (s < 3 * count + lag) & (lax.rem(s + 3 * 16 - lag, 3) == 2))
        def _():
            fn((s - lag) // 3)

    @pl.loop(0, STEPS + LAG_COL)
    def _(s):
        @pl.when(s < STEPS)
        def _():
            m = lax.rem(s, 3)
            t = chunk(s // 3)

            @pl.when(s == 0)
            def _():
                loads[0].wait()
                loads[1].wait()
                mask_cols(0, gm)

            @pl.when(s == 1)
            def _():
                loads[2].wait()
                mask_cols(1, um)

            @pl.when(s == 2)
            def _():
                loads[3].wait()
                loads[4].wait()
                mask_rows()

            @pl.when(m < 2)
            def _():
                rows = x_own[:, t].reshape(128, DIM)
                core_out[s] = product(rows, w_own[m, :, oth_cols])
                core_copy(s).start()
                part[s] = product(rows, w_own[m, :, own_cols])

            @pl.when(m == 2)
            def _():
                rows = og_own[:, t].reshape(128, DIM)
                core_out[s] = product_t(rows, wd_own[oth_cols, :])
                core_copy(s).start()
                part[s] = product_t(rows, wd_own[own_cols, :])

        @pl.when((s >= LAG_RING) & (s < STEPS + LAG_RING))
        def _():
            n = s - LAG_RING
            core_copy(n).wait_recv()
            value = part[n] + core_in[n]
            part[n] = value
            send[n] = value.astype(BF16)
            for copy in ring_early(n):
                copy.start()

        @pl.when((s >= LAG_FORWARD) & (s < STEPS + LAG_FORWARD))
        def _():
            n = s - LAG_FORWARD
            first = ring_early(n)[:2]
            onward = ring_late(n)
            first[0].wait_recv()
            send[n, piece(up, 0)] = (part[n, piece(up, 0)] + ring[R1, n].astype(F32)).astype(BF16)
            onward[0].start()
            first[1].wait_recv()
            send[n, piece(down, 1)] = (part[n, piece(down, 1)] + ring[L1, n].astype(F32)).astype(BF16)
            onward[1].start()

        @pl.when((s >= LAG_OWN) & (s < STEPS + LAG_OWN))
        def _():
            n = s - LAG_OWN
            for copy in ring_early(n)[2:] + ring_late(n):
                copy.wait_recv()
            first = part[n, piece(y, 0)] + ring[R3, n].astype(F32) + ring[L2, n].astype(F32)
            second = part[n, piece(y, 1)] + ring[L3, n].astype(F32) + ring[R2, n].astype(F32)
            sums[n, 0:ROWS] = first
            sums[n, ROWS : 2 * ROWS] = second
            z_out[n, 0:ROWS] = first.astype(BF16)
            z_out[n, ROWS : 2 * ROWS] = second.astype(BF16)
            z_copy(n).start()

        @pl.when((s >= LAG_FINAL) & (s < STEPS + LAG_FINAL))
        def _():
            n = s - LAG_FINAL
            z_copy(n).wait_recv()
            sums[n] = sums[n] + z_in[n].astype(F32)

        @pl.when(s == TURN)
        def _():
            xt[...] = x_own[...].reshape(TOK, DIM).T
            xt_copy.start()

        def pointwise(k):
            gate = sums[3 * k]
            upv = sums[3 * k + 1]
            back = sums[3 * k + 2]
            sig = jax.nn.sigmoid(gate)
            slope = sig * (1.0 + gate * (1.0 - sig))
            deltas[1, k, y, :, own_cols] = (back * upv * slope).astype(BF16)
            gather_own(y_copy(1, k))
            deltas[2, k, y, :, own_cols] = (back * gate * sig).astype(BF16)
            gather_own(y_copy(2, k))
            deltas[0, k, y, :, own_cols] = (gate * sig * upv).astype(BF16)

        def relay(k):
            gather_relay(y_copy(1, k))
            gather_relay(y_copy(2, k))
            gather_own(y_copy(0, k))

        def to_core(k):
            for m in (1, 2):
                gather_rest(y_copy(m, k))
                pair_copy(m, k, own_cols).start()
            gather_relay(y_copy(0, k))

        def grad(k):
            pair_copy(1, k, oth_cols).wait_recv()
            value = product_t(deltas[1, k].reshape(128, FF), w_own[0])
            pair_copy(2, k, oth_cols).wait_recv()
            value = value + product_t(deltas[2, k].reshape(128, FF), w_own[1])
            ig[k] = value.reshape(4, 32, DIM)
            for d in (2, 1, 3):
                x_copy(k, d).start()
            out_copy(k).start()
            gather_rest(y_copy(0, k))
            pair_copy(0, k, own_cols).start()

        def finish(k):
            pair_copy(0, k, oth_cols).wait_recv()
            hidden_store(k).start()
            reduce_col(k)

        at_chunk(s, LAG_FINAL, pointwise)
        at_chunk(s, LAG_RELAY, relay)
        at_chunk(s, LAG_CORE, to_core)
        at_chunk(s, LAG_GRAD, grad)
        at_chunk(s, LAG_COL, finish)

    total = ig_sum[...]
    for i in range(3):
        remote(ig_z.at[0], ig_in.at[i], zl_s.at[0], zl_r.at[i], core_dev).wait_recv()
        total = total + ig_in[i].astype(F32)
    ig_out[...] = total.astype(BF16)

    @pl.loop(0, STEPS)
    def _(s):
        core_copy(s).wait_send()
        for copy in ring_early(s) + ring_late(s):
            copy.wait_send()
        z_copy(s).wait_send()

    @pl.loop(0, CHUNKS)
    def _(k):
        for m in range(3):
            gather_drain(y_copy(m, k))
            pair_copy(m, k, own_cols).wait_send()
        for d in (1, 2, 3):
            x_copy(k, d).wait_send()

        @pl.when(zl != chunk(k))
        def _():
            zl_copy(k).wait_send()

        out_copy(k).wait()
        hidden_store(k).wait()

    xt_copy.wait()


def exchange(inputs, out_grad, gate_weight, up_weight, down_weight, gate_mask, up_mask, down_mask):
    any_spec = pl.BlockSpec(memory_space=pl.ANY)
    smem = pl.BlockSpec(memory_space=pltpu.SMEM)
    dma = pltpu.SemaphoreType.DMA
    return pl.pallas_call(
        exchange_kernel,
        out_shape=(
            jax.ShapeDtypeStruct((3, 4, CHUNKS, 32, FF), BF16),
            jax.ShapeDtypeStruct((DIM, TOK), BF16),
            jax.ShapeDtypeStruct((32, DIM), BF16),
        ),
        in_specs=[any_spec] * 5 + [smem] * 3,
        out_specs=(any_spec, any_spec, pl.BlockSpec(memory_space=pltpu.VMEM)),
        scratch_shapes=[
            pltpu.VMEM((4, CHUNKS, 32, DIM), BF16),
            pltpu.VMEM((4, CHUNKS, 32, DIM), BF16),
            pltpu.VMEM((DIM, TOK), BF16),
            pltpu.VMEM((2, DIM, FF), BF16),
            pltpu.VMEM((FF, DIM), BF16),
            pltpu.VMEM((STEPS, 128, HALF), F32),
            pltpu.VMEM((STEPS, 128, HALF), F32),
            pltpu.VMEM((STEPS, 128, HALF), F32),
            pltpu.VMEM((STEPS, 128, HALF), BF16),
            pltpu.VMEM((6, STEPS, ROWS, HALF), BF16),
            pltpu.VMEM((STEPS, 2 * ROWS, HALF), BF16),
            pltpu.VMEM((STEPS, 2 * ROWS, HALF), BF16),
            pltpu.VMEM((STEPS, 2 * ROWS, HALF), F32),
            pltpu.VMEM((3, CHUNKS, 4, 32, FF), BF16),
            pltpu.VMEM((CHUNKS, 4, 32, DIM), F32),
            pltpu.VMEM((CHUNKS, 3, 32, DIM), F32),
            pltpu.VMEM((CHUNKS, 32, DIM), BF16),
            pltpu.VMEM((32, DIM), F32),
            pltpu.VMEM((3, 32, DIM), BF16),
            dma((14,)),
            dma((STEPS,)),
            dma((STEPS,)),
            dma((6, STEPS)),
            dma((6, STEPS)),
            dma((STEPS,)),
            dma((STEPS,)),
            dma((3, CHUNKS, 7)),
            dma((3, CHUNKS, 7)),
            dma((CHUNKS, 3)),
            dma((CHUNKS, 3)),
            dma((CHUNKS,)),
            dma((3,)),
        ],
        compiler_params=pltpu.CompilerParams(
            collective_id=0, has_side_effects=True, vmem_limit_bytes=58 * 2**20
        ),
        name="exchange",
    )(
        inputs.reshape(4, CHUNKS, 32, DIM),
        out_grad.reshape(4, CHUNKS, 32, DIM),
        gate_weight,
        up_weight,
        down_weight,
        gate_mask,
        up_mask,
        down_mask.T,
    )


def grads_kernel(
    xt_hbm, og_hbm, d_hbm, gm, um, dm, ig_ref, gate_hbm, up_hbm, down_hbm, ig_out, xt, og, d, cols_out, rows_out, sem_in, sem_out
):
    loads = [
        pltpu.make_async_copy(xt_hbm, xt, sem_in.at[0]),
        pltpu.make_async_copy(d_hbm.at[1], d.at[1], sem_in.at[1]),
        pltpu.make_async_copy(d_hbm.at[2], d.at[2], sem_in.at[2]),
        pltpu.make_async_copy(og_hbm, og, sem_in.at[3]),
        pltpu.make_async_copy(d_hbm.at[0], d.at[0], sem_in.at[4]),
    ]
    for load in loads:
        load.start()
    ig_out[...] = ig_ref[...]
    loads[0].wait()
    stores = [
        pltpu.make_async_copy(cols_out.at[0], gate_hbm, sem_out.at[0]),
        pltpu.make_async_copy(cols_out.at[1], up_hbm, sem_out.at[1]),
    ]
    for which, mask in ((1, gm), (2, um)):
        loads[which].wait()

        @pl.loop(0, FF // 256)
        def _(j):
            value = product(xt[...], d[which, :, pl.ds(pl.multiple_of(j * 256, 256), 256)])
            for k in range(2):
                cols = pl.ds(pl.multiple_of(j * 256 + k * BLOCK, BLOCK), BLOCK)
                for i in range(DIM // BLOCK):
                    rows = slice(i * BLOCK, (i + 1) * BLOCK)
                    keep = mask[i, 2 * j + k].astype(F32)
                    part = value[rows, k * BLOCK : (k + 1) * BLOCK] * keep
                    cols_out[which - 1, rows, cols] = part.astype(BF16)

        stores[which - 1].start()
    loads[3].wait()
    loads[4].wait()

    def store_rows(j):
        rows = pl.ds(pl.multiple_of(j * 256, 256), 256)
        return pltpu.make_async_copy(rows_out.at[rows], down_hbm.at[rows], sem_out.at[2 + j])

    @pl.loop(0, FF // 256)
    def _(j):
        value = t_product(d[0, :, pl.ds(pl.multiple_of(j * 256, 256), 256)], og[...])
        for k in range(2):
            rows = pl.ds(pl.multiple_of(j * 256 + k * BLOCK, BLOCK), BLOCK)
            for i in range(DIM // BLOCK):
                cols = slice(i * BLOCK, (i + 1) * BLOCK)
                keep = dm[i, 2 * j + k].astype(F32)
                part = value[k * BLOCK : (k + 1) * BLOCK, cols] * keep
                rows_out[rows, cols] = part.astype(BF16)
        store_rows(j).start()

    for store in stores:
        store.wait()
    for j in range(FF // 256):
        store_rows(j).wait()


def grads(turned, out_grad, deltas, gate_mask, up_mask, down_mask, ig):
    any_spec = pl.BlockSpec(memory_space=pl.ANY)
    smem = pl.BlockSpec(memory_space=pltpu.SMEM)
    vmem = pl.BlockSpec(memory_space=pltpu.VMEM)
    return pl.pallas_call(
        grads_kernel,
        out_shape=(
            jax.ShapeDtypeStruct((DIM, FF), BF16),
            jax.ShapeDtypeStruct((DIM, FF), BF16),
            jax.ShapeDtypeStruct((FF, DIM), BF16),
            jax.ShapeDtypeStruct((32, DIM), BF16),
        ),
        in_specs=[any_spec, any_spec, any_spec, smem, smem, smem, vmem],
        out_specs=(any_spec, any_spec, any_spec, vmem),
        scratch_shapes=[
            pltpu.VMEM((DIM, TOK), BF16),
            pltpu.VMEM((TOK, DIM), BF16),
            pltpu.VMEM((3, TOK, FF), BF16),
            pltpu.VMEM((2, DIM, FF), BF16),
            pltpu.VMEM((FF, DIM), BF16),
            pltpu.SemaphoreType.DMA((5,)),
            pltpu.SemaphoreType.DMA((2 + FF // 256,)),
        ],
        compiler_params=pltpu.CompilerParams(vmem_limit_bytes=62 * 2**20),
        name="grads",
    )(turned, out_grad, deltas, gate_mask, up_mask, down_mask.T, ig)


def shards(inputs, out_grad, gate_weight, up_weight, down_weight, gate_mask, up_mask, down_mask):
    deltas, turned, ig = exchange(inputs, out_grad, gate_weight, up_weight, down_weight, gate_mask, up_mask, down_mask)
    deltas = deltas.reshape(3, TOK, FF)
    gate_grad, up_grad, down_grad, input_grad = grads(turned, out_grad, deltas, gate_mask, up_mask, down_mask, ig)
    return (input_grad, gate_grad, up_grad, down_grad)


def solution(mesh):
    placed = (
        P(None, "row"),
        P(None, "row"),
        P("row", "col"),
        P("row", "col"),
        P("col", "row"),
        P("row", "col"),
        P("row", "col"),
        P("col", "row"),
    )
    return jax.shard_map(
        shards,
        mesh=mesh,
        in_specs=placed,
        out_specs=(P("col", "row"), P("row", "col"), P("row", "col"), P("col", "row")),
        check_vma=False,
    )
```

time: 948 us -> 89.5 us (0.09)
  waiting for transfers between devices: 862 us -> 0 us
  Pallas kernels: 0 us -> 88.7 us
  local copies, waits for them, and re-layouts: 39.6 us -> 0 us
  matrix products: 17.3 us -> 0 us
  between operations: 14.6 us -> 0.64 us
    unnamed x6 -> x0, waiting for transfers between devices: 629 us -> none
    all_gather x3 -> x0, waiting for transfers between devices: 155 us -> none  [the longest x1 56.4 us: shards(): piece_gate = lax.all_gather(gate_delta, 'row', axis=0, tiled=True)]
    pallas_call x0 -> x2, Pallas kernels: none -> 88.7 us  [the longest x1 78.1 us: exchange(): pl.pallas_call(exchange_kernel, out_shape=(jax.ShapeDtypeStruct((3, 4, CH...]
    reduce_scatter x1 -> x0, waiting for transfers between devices: 76.9 us -> none  [shards(): lax.psum_scatter(partial_value, 'col', scatter_dimension=0, tiled=True)]
    unnamed x35 -> x0, local copies, waits for them, and re-layouts: 17.5 us -> none
    dot_general x8 -> x0, matrix products: 17.3 us -> none  [contract(): lax.dot_general(former, latter, (((former_dim,), (latter_dim,)), ((), ())...]
    another operation x1 -> x0, local copies, waits for them, and re-layouts: 15.6 us -> none  [shards(): jnp.stack([contract(rows_in, gate_full, 1, 0), contract(rows_in, up_full,...]
  transfers between devices with their start and end apart: 5 -> 0, of which waited for: 5 -> 0; matrix products, arithmetic and copies ran while one was open for 2% -> 0% of each run, Pallas kernels for 0% -> 0%
where the time goes in v2:
time: 89.5 us; the launch traced here: 89.4 us
  Pallas kernels  88.7 us (99%)
    pallas_call x1, Pallas kernels, exchange(): pl.pallas_call(exchange_kernel, out_shape=(jax.ShapeDtypeStruct((3, 4, CH...  78.1 us
    pallas_call x1, Pallas kernels, grads(): pl.pallas_call(grads_kernel, out_shape=(jax.ShapeDtypeStruct((DIM, FF), B...  10.7 us

profile of v2, /device:TPU:32, one launch (start us, length us, event | category | flops | bytes accessed | tf_op | source)
XLA Modules:
  0.0 89.4 jit_solution(5694195034872207701)
XLA Ops:
  0.6 78.1 %exchange.1 = (bf16[3,4,4,32,1792]{4,3,2,1,0:T(8,128)(2,1)}, bf16[512,512]{1,0:T(8,128)(2,1)}, bf16[32,512]{1,0:T(8,128)(2,1)}) custom-call(bf16[4,4,32,512]{3,2,1,0:T(8,128)(2,1)} %bitcast.6, bf16[4,4,32,512]{3,2,1,0:T(8,128)(2,1)} %bitcast.5, bf16[512,1792]{1,0:T(8,128)(2,1)} %wg_hbm.1, bf16[512,1792]{1,0:T(8,128)(2,1)} %wu_hbm.1, ...), custom_call_target="tpu_custom_call" | custom-call | tf_op jit(solution)/shard_map/exchange/pallas_call | solution.py:382
  78.7 10.7 %grads.1 = (bf16[512,1792]{1,0:T(8,128)(2,1)}, bf16[512,1792]{1,0:T(8,128)(2,1)}, bf16[1792,512]{1,0:T(8,128)(2,1)}, bf16[32,512]{1,0:T(8,128)(2,1)}) custom-call(bf16[512,512]{1,0:T(8,128)(2,1)} %get-tuple-element.11.xt_hbm, bf16[512,512]{1,0:T(8,128)(2,1)} %og_hbm.1, bf16[3,512,1792]{2,1,0:T(8,128)(2,1)} %bitcast.4, s32[4,14]{1,0:T(4,128)} %gm.3, ...), custom_call_target="tpu_custom_call" | custom-call | tf_op jit(solution)/shard_map/grads/pallas_call | solution.py:503

commit v3 on v2

--- a/solution.py
+++ b/solution.py
@@ -14,17 +14,19 @@
 FF = 1792
 HALF = FF // 2
 CHUNKS = 4
-ROWS = 16
+ROWS = 64 // CHUNKS
+GROUP = 2 * ROWS
+SPAN = 4 * GROUP
 STEPS = 3 * CHUNKS
 
 LAG_RING = 1
 LAG_FORWARD = 3
 LAG_OWN = 5
-LAG_FINAL = 9
-LAG_RELAY = 11
-LAG_CORE = 13
-LAG_GRAD = 14
-LAG_COL = 16
+LAG_FINAL = 8
+LAG_RELAY = 10
+LAG_CORE = 12
+LAG_GRAD = 13
+LAG_COL = 15
 TURN = 13
 
 R1, R2, R3, L1, L2, L3 = range(6)
@@ -80,17 +82,21 @@
         )
 
     def chunk(k):
-        return lax.rem(k + 2, 4)
+        return lax.rem(k + CHUNKS // 2, CHUNKS)
+
+    def owner(k):
+        return chunk(k) // (CHUNKS // 4)
 
     def piece(yy, hh):
-        return pl.ds(pl.multiple_of(yy * 32 + hh * ROWS, ROWS), ROWS)
+        return pl.ds(pl.multiple_of(yy * GROUP + hh * ROWS, ROWS), ROWS)
 
     def half(hh):
         return pl.ds(pl.multiple_of(hh * ROWS, ROWS), ROWS)
 
     loads = [
         pltpu.make_async_copy(x_hbm, x_own, local_sem.at[0]),
-        pltpu.make_async_copy(wg_hbm, w_own.at[0], local_sem.at[1]),
+        pltpu.make_async_copy(wg_hbm.at[:, oth_cols], w_own.at[0, :, oth_cols], local_sem.at[1]),
+        pltpu.make_async_copy(wg_hbm.at[:, own_cols], w_own.at[0, :, own_cols], local_sem.at[5]),
         pltpu.make_async_copy(wu_hbm, w_own.at[1], local_sem.at[2]),
         pltpu.make_async_copy(og_hbm, og_own, local_sem.at[3]),
         pltpu.make_async_copy(wd_hbm, wd_own, local_sem.at[4]),
@@ -105,9 +111,10 @@
         pl.semaphore_signal(bar, inc=1, device_id=dev, device_id_type=MESH)
     pl.semaphore_wait(bar, len(friends))
 
-    def mask_cols(which, mask_ref):
-        @pl.loop(0, FF // BLOCK)
-        def _(j):
+    def mask_cols(which, mask_ref, first, count):
+        @pl.loop(0, count * HALF // BLOCK)
+        def _(n):
+            j = first * (HALF // BLOCK) + n
             cols = pl.ds(pl.multiple_of(j * BLOCK, BLOCK), BLOCK)
             for i in range(DIM // BLOCK):
                 rows = pl.ds(i * BLOCK, BLOCK)
@@ -150,11 +157,13 @@
         ref = deltas.at[m, k, :, :, cols]
         return remote(ref, ref, ag_s.at[m, k, 6], ag_r.at[m, k, 6], core_dev)
 
-    def gather_own(copy):
-        copy(0, y, 0, right).start()
-        copy(3, y, 1, left).start()
-        copy(1, y, 1, right).start()
-        copy(2, y, 0, left).start()
+    def gather_own(*copies):
+        for copy in copies:
+            copy(0, y, 0, right).start()
+            copy(3, y, 1, left).start()
+        for copy in copies:
+            copy(1, y, 1, right).start()
+            copy(2, y, 0, left).start()
 
     def gather_relay(copy):
         copy(0, down, 0, right).wait_recv()
@@ -177,13 +186,13 @@
 
     def out_copy(k):
         return pltpu.make_async_copy(
-            deltas.at[pl.ds(1, 2), k], d_hbm.at[pl.ds(1, 2), :, chunk(k)], local_sem.at[5 + k]
+            deltas.at[pl.ds(1, 2), k], d_hbm.at[pl.ds(1, 2), :, chunk(k)], local_sem.at[7 + k]
         )
 
     def hidden_store(k):
-        return pltpu.make_async_copy(deltas.at[0, k], d_hbm.at[0, :, chunk(k)], local_sem.at[10 + k])
-
-    xt_copy = pltpu.make_async_copy(xt, xt_hbm, local_sem.at[9])
+        return pltpu.make_async_copy(deltas.at[0, k], d_hbm.at[0, :, chunk(k)], local_sem.at[7 + CHUNKS + k])
+
+    xt_copy = pltpu.make_async_copy(xt, xt_hbm, local_sem.at[6])
 
     def x_copy(k, d):
         return remote(
@@ -191,8 +200,11 @@
         )
 
     def zl_copy(k):
-        slot = lax.rem(zl - chunk(k) + 7, 4)
-        return remote(ig_z.at[k], ig_in.at[slot], zl_s.at[k], zl_r.at[slot], (row, x * 4 + chunk(k)))
+        slot = lax.rem(zl - owner(k) + 7, 4)
+        part_of = lax.rem(chunk(k), CHUNKS // 4)
+        return remote(
+            ig_z.at[k], ig_in.at[part_of, slot], zl_s.at[k], zl_r.at[part_of, slot], (row, x * 4 + owner(k))
+        )
 
     def reduce_col(k):
         total = ig[k, x]
@@ -200,17 +212,31 @@
             x_copy(k, d).wait_recv()
             total = total + ig_x[k, d - 1]
 
-        @pl.when(zl == chunk(k))
-        def _():
-            ig_sum[...] = total
-
-        @pl.when(zl != chunk(k))
+        @pl.when(zl == owner(k))
+        def _():
+            ig_sum[lax.rem(chunk(k), CHUNKS // 4)] = total
+
+        @pl.when(zl != owner(k))
         def _():
             ig_z[k] = total.astype(BF16)
             zl_copy(k).start()
 
+    def drain(k):
+        for m in range(3):
+            gather_drain(y_copy(m, k))
+            pair_copy(m, k, own_cols).wait_send()
+        for d in (1, 2, 3):
+            x_copy(k, d).wait_send()
+
+        @pl.when(zl != owner(k))
+        def _():
+            zl_copy(k).wait_send()
+
+        out_copy(k).wait()
+        hidden_store(k).wait()
+
     def at_chunk(s, lag, fn, count=CHUNKS):
-        @pl.when((s >= lag + 2) & (s < 3 * count + lag) & (lax.rem(s + 3 * 16 - lag, 3) == 2))
+        @pl.when((s >= lag + 2) & (s < 3 * count + lag) & (lax.rem(s + 3 * 32 - lag, 3) == 2))
         def _():
             fn((s - lag) // 3)
 
@@ -225,29 +251,35 @@
             def _():
                 loads[0].wait()
                 loads[1].wait()
-                mask_cols(0, gm)
+                mask_cols(0, gm, 1 - c, 1)
 
             @pl.when(s == 1)
             def _():
-                loads[2].wait()
-                mask_cols(1, um)
+                loads[3].wait()
+                mask_cols(1, um, 0, 2)
 
             @pl.when(s == 2)
             def _():
-                loads[3].wait()
                 loads[4].wait()
+                loads[5].wait()
                 mask_rows()
 
             @pl.when(m < 2)
             def _():
-                rows = x_own[:, t].reshape(128, DIM)
+                rows = x_own[:, t].reshape(SPAN, DIM)
                 core_out[s] = product(rows, w_own[m, :, oth_cols])
                 core_copy(s).start()
+
+                @pl.when(s == 0)
+                def _():
+                    loads[2].wait()
+                    mask_cols(0, gm, c, 1)
+
                 part[s] = product(rows, w_own[m, :, own_cols])
 
             @pl.when(m == 2)
             def _():
-                rows = og_own[:, t].reshape(128, DIM)
+                rows = og_own[:, t].reshape(SPAN, DIM)
                 core_out[s] = product_t(rows, wd_own[oth_cols, :])
                 core_copy(s).start()
                 part[s] = product_t(rows, wd_own[own_cols, :])
@@ -292,6 +324,10 @@
             n = s - LAG_FINAL
             z_copy(n).wait_recv()
             sums[n] = sums[n] + z_in[n].astype(F32)
+            core_copy(n).wait_send()
+            for copy in ring_early(n) + ring_late(n):
+                copy.wait_send()
+            z_copy(n).wait_send()
 
         @pl.when(s == TURN)
         def _():
@@ -305,9 +341,8 @@
             sig = jax.nn.sigmoid(gate)
             slope = sig * (1.0 + gate * (1.0 - sig))
             deltas[1, k, y, :, own_cols] = (back * upv * slope).astype(BF16)
-            gather_own(y_copy(1, k))
             deltas[2, k, y, :, own_cols] = (back * gate * sig).astype(BF16)
-            gather_own(y_copy(2, k))
+            gather_own(y_copy(1, k), y_copy(2, k))
             deltas[0, k, y, :, own_cols] = (gate * sig * upv).astype(BF16)
 
         def relay(k):
@@ -323,10 +358,10 @@
 
         def grad(k):
             pair_copy(1, k, oth_cols).wait_recv()
-            value = product_t(deltas[1, k].reshape(128, FF), w_own[0])
+            value = product_t(deltas[1, k].reshape(SPAN, FF), w_own[0])
             pair_copy(2, k, oth_cols).wait_recv()
-            value = value + product_t(deltas[2, k].reshape(128, FF), w_own[1])
-            ig[k] = value.reshape(4, 32, DIM)
+            value = value + product_t(deltas[2, k].reshape(SPAN, FF), w_own[1])
+            ig[k] = value.reshape(4, GROUP, DIM)
             for d in (2, 1, 3):
                 x_copy(k, d).start()
             out_copy(k).start()
@@ -338,40 +373,26 @@
             hidden_store(k).start()
             reduce_col(k)
 
+            @pl.when(k > 0)
+            def _():
+                drain(k - 1)
+
         at_chunk(s, LAG_FINAL, pointwise)
         at_chunk(s, LAG_RELAY, relay)
         at_chunk(s, LAG_CORE, to_core)
         at_chunk(s, LAG_GRAD, grad)
         at_chunk(s, LAG_COL, finish)
 
-    total = ig_sum[...]
-    for i in range(3):
-        remote(ig_z.at[0], ig_in.at[i], zl_s.at[0], zl_r.at[i], core_dev).wait_recv()
-        total = total + ig_in[i].astype(F32)
-    ig_out[...] = total.astype(BF16)
-
-    @pl.loop(0, STEPS)
-    def _(s):
-        core_copy(s).wait_send()
-        for copy in ring_early(s) + ring_late(s):
-            copy.wait_send()
-        z_copy(s).wait_send()
-
-    @pl.loop(0, CHUNKS)
-    def _(k):
-        for m in range(3):
-            gather_drain(y_copy(m, k))
-            pair_copy(m, k, own_cols).wait_send()
-        for d in (1, 2, 3):
-            x_copy(k, d).wait_send()
-
-        @pl.when(zl != chunk(k))
-        def _():
-            zl_copy(k).wait_send()
-
-        out_copy(k).wait()
-        hidden_store(k).wait()
-
+    for part_of in range(CHUNKS // 4):
+        total = ig_sum[part_of]
+        for i in range(3):
+            remote(
+                ig_z.at[0], ig_in.at[part_of, i], zl_s.at[0], zl_r.at[part_of, i], core_dev
+            ).wait_recv()
+            total = total + ig_in[part_of, i].astype(F32)
+        ig_out[pl.ds(part_of * GROUP, GROUP)] = total.astype(BF16)
+
+    drain(CHUNKS - 1)
     xt_copy.wait()
 
 
@@ -382,33 +403,33 @@
     return pl.pallas_call(
         exchange_kernel,
         out_shape=(
-            jax.ShapeDtypeStruct((3, 4, CHUNKS, 32, FF), BF16),
+            jax.ShapeDtypeStruct((3, 4, CHUNKS, GROUP, FF), BF16),
             jax.ShapeDtypeStruct((DIM, TOK), BF16),
             jax.ShapeDtypeStruct((32, DIM), BF16),
         ),
         in_specs=[any_spec] * 5 + [smem] * 3,
         out_specs=(any_spec, any_spec, pl.BlockSpec(memory_space=pltpu.VMEM)),
         scratch_shapes=[
-            pltpu.VMEM((4, CHUNKS, 32, DIM), BF16),
-            pltpu.VMEM((4, CHUNKS, 32, DIM), BF16),
+            pltpu.VMEM((4, CHUNKS, GROUP, DIM), BF16),
+            pltpu.VMEM((4, CHUNKS, GROUP, DIM), BF16),
             pltpu.VMEM((DIM, TOK), BF16),
             pltpu.VMEM((2, DIM, FF), BF16),
             pltpu.VMEM((FF, DIM), BF16),
-            pltpu.VMEM((STEPS, 128, HALF), F32),
-            pltpu.VMEM((STEPS, 128, HALF), F32),
-            pltpu.VMEM((STEPS, 128, HALF), F32),
-            pltpu.VMEM((STEPS, 128, HALF), BF16),
+            pltpu.VMEM((STEPS, SPAN, HALF), F32),
+            pltpu.VMEM((STEPS, SPAN, HALF), F32),
+            pltpu.VMEM((STEPS, SPAN, HALF), F32),
+            pltpu.VMEM((STEPS, SPAN, HALF), BF16),
             pltpu.VMEM((6, STEPS, ROWS, HALF), BF16),
             pltpu.VMEM((STEPS, 2 * ROWS, HALF), BF16),
             pltpu.VMEM((STEPS, 2 * ROWS, HALF), BF16),
             pltpu.VMEM((STEPS, 2 * ROWS, HALF), F32),
-            pltpu.VMEM((3, CHUNKS, 4, 32, FF), BF16),
-            pltpu.VMEM((CHUNKS, 4, 32, DIM), F32),
-            pltpu.VMEM((CHUNKS, 3, 32, DIM), F32),
-            pltpu.VMEM((CHUNKS, 32, DIM), BF16),
-            pltpu.VMEM((32, DIM), F32),
-            pltpu.VMEM((3, 32, DIM), BF16),
-            dma((14,)),
+            pltpu.VMEM((3, CHUNKS, 4, GROUP, FF), BF16),
+            pltpu.VMEM((CHUNKS, 4, GROUP, DIM), F32),
+            pltpu.VMEM((CHUNKS, 3, GROUP, DIM), F32),
+            pltpu.VMEM((CHUNKS, GROUP, DIM), BF16),
+            pltpu.VMEM((CHUNKS // 4, GROUP, DIM), F32),
+            pltpu.VMEM((CHUNKS // 4, 3, GROUP, DIM), BF16),
+            dma((7 + 2 * CHUNKS,)),
             dma((STEPS,)),
             dma((STEPS,)),
             dma((6, STEPS)),
@@ -420,15 +441,15 @@
             dma((CHUNKS, 3)),
             dma((CHUNKS, 3)),
             dma((CHUNKS,)),
-            dma((3,)),
+            dma((CHUNKS // 4, 3)),
         ],
         compiler_params=pltpu.CompilerParams(
             collective_id=0, has_side_effects=True, vmem_limit_bytes=58 * 2**20
         ),
         name="exchange",
     )(
-        inputs.reshape(4, CHUNKS, 32, DIM),
-        out_grad.reshape(4, CHUNKS, 32, DIM),
+        inputs.reshape(4, CHUNKS, GROUP, DIM),
+        out_grad.reshape(4, CHUNKS, GROUP, DIM),
         gate_weight,
         up_weight,
         down_weight,
@@ -459,11 +480,10 @@
     for which, mask in ((1, gm), (2, um)):
         loads[which].wait()
 
-        @pl.loop(0, FF // 256)
-        def _(j):
-            value = product(xt[...], d[which, :, pl.ds(pl.multiple_of(j * 256, 256), 256)])
+        for j in range(FF // 256):
+            value = product(xt[...], d[which, :, j * 256 : (j + 1) * 256])
             for k in range(2):
-                cols = pl.ds(pl.multiple_of(j * 256 + k * BLOCK, BLOCK), BLOCK)
+                cols = pl.ds(j * 256 + k * BLOCK, BLOCK)
                 for i in range(DIM // BLOCK):
                     rows = slice(i * BLOCK, (i + 1) * BLOCK)
                     keep = mask[i, 2 * j + k].astype(F32)
@@ -475,14 +495,13 @@
     loads[4].wait()
 
     def store_rows(j):
-        rows = pl.ds(pl.multiple_of(j * 256, 256), 256)
+        rows = pl.ds(j * 256, 256)
         return pltpu.make_async_copy(rows_out.at[rows], down_hbm.at[rows], sem_out.at[2 + j])
 
-    @pl.loop(0, FF // 256)
-    def _(j):
-        value = t_product(d[0, :, pl.ds(pl.multiple_of(j * 256, 256), 256)], og[...])
+    for j in range(FF // 256):
+        value = t_product(d[0, :, j * 256 : (j + 1) * 256], og[...])
         for k in range(2):
-            rows = pl.ds(pl.multiple_of(j * 256 + k * BLOCK, BLOCK), BLOCK)
+            rows = pl.ds(j * 256 + k * BLOCK, BLOCK)
             for i in range(DIM // BLOCK):
                 cols = slice(i * BLOCK, (i + 1) * BLOCK)
                 keep = dm[i, 2 * j + k].astype(F32)

time: 89.5 us -> 85.7 us (0.958)
  Pallas kernels: 88.7 us -> 84.9 us
    pallas_call x1, Pallas kernels: 10.7 us -> 7.54 us  [grads(): pl.pallas_call(grads_kernel, out_shape=(jax.ShapeDtypeStruct((DIM, FF), B...]
where the time goes in v3:
time: 85.7 us; the launch traced here: 85.5 us
  Pallas kernels  84.9 us (99%)
    pallas_call x1, Pallas kernels, exchange(): pl.pallas_call(exchange_kernel, out_shape=(jax.ShapeDtypeStruct((3, 4, CH...  77.4 us
    pallas_call x1, Pallas kernels, grads(): pl.pallas_call(grads_kernel, out_shape=(jax.ShapeDtypeStruct((DIM, FF), B...  7.54 us

profile of v3, /device:TPU:32, one launch (start us, length us, event | category | flops | bytes accessed | tf_op | source)
XLA Modules:
  0.0 85.5 jit_solution(9116520147421449199)
XLA Ops:
  0.6 77.4 %exchange.1 = (bf16[3,4,4,32,1792]{4,3,2,1,0:T(8,128)(2,1)}, bf16[512,512]{1,0:T(8,128)(2,1)}, bf16[32,512]{1,0:T(8,128)(2,1)}) custom-call(bf16[4,4,32,512]{3,2,1,0:T(8,128)(2,1)} %bitcast.6, bf16[4,4,32,512]{3,2,1,0:T(8,128)(2,1)} %bitcast.5, bf16[512,1792]{1,0:T(8,128)(2,1)} %wg_hbm.1, bf16[512,1792]{1,0:T(8,128)(2,1)} %wu_hbm.1, ...), custom_call_target="tpu_custom_call" | custom-call | tf_op jit(solution)/shard_map/exchange/pallas_call | solution.py:403
  78.0 7.5 %grads.1 = (bf16[512,1792]{1,0:T(8,128)(2,1)}, bf16[512,1792]{1,0:T(8,128)(2,1)}, bf16[1792,512]{1,0:T(8,128)(2,1)}, bf16[32,512]{1,0:T(8,128)(2,1)}) custom-call(bf16[512,512]{1,0:T(8,128)(2,1)} %get-tuple-element.11.xt_hbm, bf16[512,512]{1,0:T(8,128)(2,1)} %og_hbm.1, bf16[3,512,1792]{2,1,0:T(8,128)(2,1)} %bitcast.4, s32[4,14]{1,0:T(4,128)} %gm.3, ...), custom_call_target="tpu_custom_call" | custom-call | tf_op jit(solution)/shard_map/grads/pallas_call | solution.py:522

commit v4 on v3

--- a/solution.py
+++ b/solution.py
@@ -45,12 +45,12 @@
 
 
 def exchange_kernel(
-    x_hbm, og_hbm, wg_hbm, wu_hbm, wd_hbm, gm, um, dm,
+    x_hbm, og_hbm, wg_hbm, wu_hbm, wd_hbm, gm_hbm, um_hbm, dm_hbm,
     d_hbm, xt_hbm, ig_out,
-    x_own, og_own, xt, w_own, wd_own, core_out, core_in,
+    gm, um, dm, x_own, og_own, xt, w_own, wd_own, core_out, core_in,
     part, send, ring, z_out, z_in, sums, deltas,
     ig, ig_x, ig_z, ig_sum, ig_in,
-    local_sem, core_s, core_r, ring_s, ring_r, z_s, z_r, ag_s, ag_r, x_s, x_r, zl_s, zl_r,
+    local_sem, mask_sem, core_s, core_r, ring_s, ring_r, z_s, z_r, ag_s, ag_r, x_s, x_r, zl_s, zl_r,
 ):
     row = lax.axis_index("row")
     col = lax.axis_index("col")
@@ -101,7 +101,12 @@
         pltpu.make_async_copy(og_hbm, og_own, local_sem.at[3]),
         pltpu.make_async_copy(wd_hbm, wd_own, local_sem.at[4]),
     ]
-    for load in loads:
+    masks = [
+        pltpu.make_async_copy(gm_hbm, gm, mask_sem.at[0]),
+        pltpu.make_async_copy(um_hbm, um, mask_sem.at[1]),
+        pltpu.make_async_copy(dm_hbm, dm, mask_sem.at[2]),
+    ]
+    for load in loads[:2] + masks + loads[2:]:
         load.start()
 
     bar = pltpu.get_barrier_semaphore()
@@ -251,17 +256,20 @@
             def _():
                 loads[0].wait()
                 loads[1].wait()
+                masks[0].wait()
                 mask_cols(0, gm, 1 - c, 1)
 
             @pl.when(s == 1)
             def _():
                 loads[3].wait()
+                masks[1].wait()
                 mask_cols(1, um, 0, 2)
 
             @pl.when(s == 2)
             def _():
                 loads[4].wait()
                 loads[5].wait()
+                masks[2].wait()
                 mask_rows()
 
             @pl.when(m < 2)
@@ -398,7 +406,7 @@
 
 def exchange(inputs, out_grad, gate_weight, up_weight, down_weight, gate_mask, up_mask, down_mask):
     any_spec = pl.BlockSpec(memory_space=pl.ANY)
-    smem = pl.BlockSpec(memory_space=pltpu.SMEM)
+    small = pltpu.SMEM((DIM // BLOCK, FF // BLOCK), jnp.int32)
     dma = pltpu.SemaphoreType.DMA
     return pl.pallas_call(
         exchange_kernel,
@@ -407,9 +415,12 @@
             jax.ShapeDtypeStruct((DIM, TOK), BF16),
             jax.ShapeDtypeStruct((32, DIM), BF16),
         ),
-        in_specs=[any_spec] * 5 + [smem] * 3,
+        in_specs=[any_spec] * 8,
         out_specs=(any_spec, any_spec, pl.BlockSpec(memory_space=pltpu.VMEM)),
         scratch_shapes=[
+            small,
+            small,
+            small,
             pltpu.VMEM((4, CHUNKS, GROUP, DIM), BF16),
             pltpu.VMEM((4, CHUNKS, GROUP, DIM), BF16),
             pltpu.VMEM((DIM, TOK), BF16),
@@ -430,6 +441,7 @@
             pltpu.VMEM((CHUNKS // 4, GROUP, DIM), F32),
             pltpu.VMEM((CHUNKS // 4, 3, GROUP, DIM), BF16),
             dma((7 + 2 * CHUNKS,)),
+            dma((3,)),
             dma((STEPS,)),
             dma((STEPS,)),
             dma((6, STEPS)),
@@ -460,27 +472,40 @@
 
 
 def grads_kernel(
-    xt_hbm, og_hbm, d_hbm, gm, um, dm, ig_ref, gate_hbm, up_hbm, down_hbm, ig_out, xt, og, d, cols_out, rows_out, sem_in, sem_out
+    xt_hbm, og_hbm, d_hbm, gm_hbm, um_hbm, dm_hbm, ig_hbm,
+    gate_hbm, up_hbm, down_hbm, ig_out_hbm,
+    gm, um, dm, ig, xt, og, d, cols_out, rows_out, sem_in, sem_out,
 ):
+    head = pl.ds(0, 768)
+    tail = pl.ds(768, FF - 768)
     loads = [
         pltpu.make_async_copy(xt_hbm, xt, sem_in.at[0]),
-        pltpu.make_async_copy(d_hbm.at[1], d.at[1], sem_in.at[1]),
-        pltpu.make_async_copy(d_hbm.at[2], d.at[2], sem_in.at[2]),
-        pltpu.make_async_copy(og_hbm, og, sem_in.at[3]),
-        pltpu.make_async_copy(d_hbm.at[0], d.at[0], sem_in.at[4]),
+        pltpu.make_async_copy(d_hbm.at[1, :, head], d.at[1, :, head], sem_in.at[1]),
+        pltpu.make_async_copy(gm_hbm, gm, sem_in.at[2]),
+        pltpu.make_async_copy(d_hbm.at[1, :, tail], d.at[1, :, tail], sem_in.at[3]),
+        pltpu.make_async_copy(um_hbm, um, sem_in.at[4]),
+        pltpu.make_async_copy(d_hbm.at[2], d.at[2], sem_in.at[5]),
+        pltpu.make_async_copy(dm_hbm, dm, sem_in.at[6]),
+        pltpu.make_async_copy(ig_hbm, ig, sem_in.at[7]),
+        pltpu.make_async_copy(og_hbm, og, sem_in.at[8]),
+        pltpu.make_async_copy(d_hbm.at[0], d.at[0], sem_in.at[9]),
     ]
     for load in loads:
         load.start()
-    ig_out[...] = ig_ref[...]
-    loads[0].wait()
+    for load in loads[:3]:
+        load.wait()
+    ig_store = pltpu.make_async_copy(ig, ig_out_hbm, sem_out.at[2 + FF // 256])
     stores = [
         pltpu.make_async_copy(cols_out.at[0], gate_hbm, sem_out.at[0]),
         pltpu.make_async_copy(cols_out.at[1], up_hbm, sem_out.at[1]),
     ]
     for which, mask in ((1, gm), (2, um)):
-        loads[which].wait()
-
+        if which == 2:
+            loads[4].wait()
+            loads[5].wait()
         for j in range(FF // 256):
+            if which == 1 and j == 3:
+                loads[3].wait()
             value = product(xt[...], d[which, :, j * 256 : (j + 1) * 256])
             for k in range(2):
                 cols = pl.ds(j * 256 + k * BLOCK, BLOCK)
@@ -491,8 +516,9 @@
                     cols_out[which - 1, rows, cols] = part.astype(BF16)
 
         stores[which - 1].start()
-    loads[3].wait()
-    loads[4].wait()
+    for load in loads[6:]:
+        load.wait()
+    ig_store.start()
 
     def store_rows(j):
         rows = pl.ds(j * 256, 256)
@@ -509,6 +535,7 @@
                 rows_out[rows, cols] = part.astype(BF16)
         store_rows(j).start()
 
+    ig_store.wait()
     for store in stores:
         store.wait()
     for j in range(FF // 256):
@@ -517,8 +544,7 @@
 
 def grads(turned, out_grad, deltas, gate_mask, up_mask, down_mask, ig):
     any_spec = pl.BlockSpec(memory_space=pl.ANY)
-    smem = pl.BlockSpec(memory_space=pltpu.SMEM)
-    vmem = pl.BlockSpec(memory_space=pltpu.VMEM)
+    small = pltpu.SMEM((DIM // BLOCK, FF // BLOCK), jnp.int32)
     return pl.pallas_call(
         grads_kernel,
         out_shape=(
@@ -527,16 +553,20 @@
             jax.ShapeDtypeStruct((FF, DIM), BF16),
             jax.ShapeDtypeStruct((32, DIM), BF16),
         ),
-        in_specs=[any_spec, any_spec, any_spec, smem, smem, smem, vmem],
-        out_specs=(any_spec, any_spec, any_spec, vmem),
+        in_specs=[any_spec] * 7,
+        out_specs=(any_spec,) * 4,
         scratch_shapes=[
+            small,
+            small,
+            small,
+            pltpu.VMEM((32, DIM), BF16),
             pltpu.VMEM((DIM, TOK), BF16),
             pltpu.VMEM((TOK, DIM), BF16),
             pltpu.VMEM((3, TOK, FF), BF16),
             pltpu.VMEM((2, DIM, FF), BF16),
             pltpu.VMEM((FF, DIM), BF16),
-            pltpu.SemaphoreType.DMA((5,)),
-            pltpu.SemaphoreType.DMA((2 + FF // 256,)),
+            pltpu.SemaphoreType.DMA((10,)),
+            pltpu.SemaphoreType.DMA((3 + FF // 256,)),
         ],
         compiler_params=pltpu.CompilerParams(vmem_limit_bytes=62 * 2**20),
         name="grads",

time: 85.7 us -> 83.4 us (0.973)
  Pallas kernels: 84.9 us -> 82.7 us
    pallas_call x1, Pallas kernels: 7.54 us -> 6.02 us  [grads(): pl.pallas_call(grads_kernel, out_shape=(jax.ShapeDtypeStruct((DIM, FF), B...]
where the time goes in v4:
time: 83.4 us
  Pallas kernels  82.7 us (99%)
    pallas_call x1, Pallas kernels, exchange(): pl.pallas_call(exchange_kernel, out_shape=(jax.ShapeDtypeStruct((3, 4, CH...  76.7 us
    pallas_call x1, Pallas kernels, grads(): pl.pallas_call(grads_kernel, out_shape=(jax.ShapeDtypeStruct((DIM, FF), B...  6.02 us

profile of v4, /device:TPU:32, one launch (start us, length us, event | category | flops | bytes accessed | tf_op | source)
XLA Modules:
  0.0 83.4 jit_solution(18173562792965392495)
XLA Ops:
  0.6 76.7 %exchange.1 = (bf16[3,4,4,32,1792]{4,3,2,1,0:T(8,128)(2,1)}, bf16[512,512]{1,0:T(8,128)(2,1)}, bf16[32,512]{1,0:T(8,128)(2,1)}) custom-call(bf16[4,4,32,512]{3,2,1,0:T(8,128)(2,1)} %bitcast.6, bf16[4,4,32,512]{3,2,1,0:T(8,128)(2,1)} %bitcast.5, bf16[512,1792]{1,0:T(8,128)(2,1)} %wg_hbm.1, bf16[512,1792]{1,0:T(8,128)(2,1)} %wu_hbm.1, ...), custom_call_target="tpu_custom_call" | custom-call | tf_op jit(solution)/shard_map/exchange/pallas_call | solution.py:411
  77.3 6.0 %grads.1 = (bf16[512,1792]{1,0:T(8,128)(2,1)}, bf16[512,1792]{1,0:T(8,128)(2,1)}, bf16[1792,512]{1,0:T(8,128)(2,1)}, bf16[32,512]{1,0:T(8,128)(2,1)}) custom-call(bf16[512,512]{1,0:T(8,128)(2,1)} %get-tuple-element.11.xt_hbm, bf16[512,512]{1,0:T(8,128)(2,1)} %og_hbm.1, bf16[3,512,1792]{2,1,0:T(8,128)(2,1)} %bitcast.4, s32[4,14]{1,0:T(4,128)} %gm_hbm.3, ...), custom_call_target="tpu_custom_call" | custom-call | tf_op jit(solution)/shard_map/grads/pallas_call | solution.py:548

commit v5 on v4

--- a/solution.py
+++ b/solution.py
@@ -17,6 +17,7 @@
 ROWS = 64 // CHUNKS
 GROUP = 2 * ROWS
 SPAN = 4 * GROUP
+PARTS = 1
 STEPS = 3 * CHUNKS
 
 LAG_RING = 1
@@ -199,43 +200,57 @@
 
     xt_copy = pltpu.make_async_copy(xt, xt_hbm, local_sem.at[6])
 
-    def x_copy(k, d):
+    def span(part):
+        return pl.ds(part * (DIM // PARTS), DIM // PARTS)
+
+    def x_copy(k, d, part):
         return remote(
-            ig.at[k, lax.rem(x + d, 4)], ig_x.at[k, d - 1], x_s.at[k, d - 1], x_r.at[k, d - 1], x_dev(d)
+            ig.at[k, lax.rem(x + d, 4), :, span(part)],
+            ig_x.at[k, d - 1, :, span(part)],
+            x_s.at[k, d - 1, part],
+            x_r.at[k, d - 1, part],
+            x_dev(d),
         )
 
-    def zl_copy(k):
+    def zl_copy(k, part):
         slot = lax.rem(zl - owner(k) + 7, 4)
         part_of = lax.rem(chunk(k), CHUNKS // 4)
         return remote(
-            ig_z.at[k], ig_in.at[part_of, slot], zl_s.at[k], zl_r.at[part_of, slot], (row, x * 4 + owner(k))
+            ig_z.at[k, :, span(part)],
+            ig_in.at[part_of, slot, :, span(part)],
+            zl_s.at[k, part],
+            zl_r.at[part_of, slot, part],
+            (row, x * 4 + owner(k)),
         )
 
     def reduce_col(k):
-        total = ig[k, x]
-        for d in (1, 2, 3):
-            x_copy(k, d).wait_recv()
-            total = total + ig_x[k, d - 1]
-
-        @pl.when(zl == owner(k))
-        def _():
-            ig_sum[lax.rem(chunk(k), CHUNKS // 4)] = total
-
-        @pl.when(zl != owner(k))
-        def _():
-            ig_z[k] = total.astype(BF16)
-            zl_copy(k).start()
+        for part in range(PARTS):
+            total = ig[k, x, :, span(part)]
+            for d in (1, 2, 3):
+                x_copy(k, d, part).wait_recv()
+                total = total + ig_x[k, d - 1, :, span(part)]
+
+            @pl.when(zl == owner(k))
+            def _():
+                ig_sum[lax.rem(chunk(k), CHUNKS // 4), :, span(part)] = total
+
+            @pl.when(zl != owner(k))
+            def _():
+                ig_z[k, :, span(part)] = total.astype(BF16)
+                zl_copy(k, part).start()
 
     def drain(k):
         for m in range(3):
             gather_drain(y_copy(m, k))
             pair_copy(m, k, own_cols).wait_send()
-        for d in (1, 2, 3):
-            x_copy(k, d).wait_send()
+        for part in range(PARTS):
+            for d in (1, 2, 3):
+                x_copy(k, d, part).wait_send()
 
         @pl.when(zl != owner(k))
         def _():
-            zl_copy(k).wait_send()
+            for part in range(PARTS):
+                zl_copy(k, part).wait_send()
 
         out_copy(k).wait()
         hidden_store(k).wait()
@@ -358,20 +373,26 @@
             gather_relay(y_copy(2, k))
             gather_own(y_copy(0, k))
 
+        def hidden_half(k, cols, rows):
+            return product_t(deltas[1, k, :, :, cols].reshape(SPAN, HALF), w_own[0, rows, cols]) + product_t(
+                deltas[2, k, :, :, cols].reshape(SPAN, HALF), w_own[1, rows, cols]
+            )
+
         def to_core(k):
             for m in (1, 2):
                 gather_rest(y_copy(m, k))
                 pair_copy(m, k, own_cols).start()
+            ig[k] = hidden_half(k, own_cols, pl.ds(0, DIM)).reshape(4, GROUP, DIM)
             gather_relay(y_copy(0, k))
 
         def grad(k):
             pair_copy(1, k, oth_cols).wait_recv()
-            value = product_t(deltas[1, k].reshape(SPAN, FF), w_own[0])
             pair_copy(2, k, oth_cols).wait_recv()
-            value = value + product_t(deltas[2, k].reshape(SPAN, FF), w_own[1])
-            ig[k] = value.reshape(4, GROUP, DIM)
-            for d in (2, 1, 3):
-                x_copy(k, d).start()
+            for part in range(PARTS):
+                value = hidden_half(k, oth_cols, span(part)).reshape(4, GROUP, DIM // PARTS)
+                ig[k, :, :, span(part)] = ig[k, :, :, span(part)] + value
+                for d in (2, 1, 3):
+                    x_copy(k, d, part).start()
             out_copy(k).start()
             gather_rest(y_copy(0, k))
             pair_copy(0, k, own_cols).start()
@@ -392,13 +413,18 @@
         at_chunk(s, LAG_COL, finish)
 
     for part_of in range(CHUNKS // 4):
-        total = ig_sum[part_of]
-        for i in range(3):
-            remote(
-                ig_z.at[0], ig_in.at[part_of, i], zl_s.at[0], zl_r.at[part_of, i], core_dev
-            ).wait_recv()
-            total = total + ig_in[part_of, i].astype(F32)
-        ig_out[pl.ds(part_of * GROUP, GROUP)] = total.astype(BF16)
+        for part in range(PARTS):
+            total = ig_sum[part_of, :, span(part)]
+            for i in range(3):
+                remote(
+                    ig_z.at[0, :, span(part)],
+                    ig_in.at[part_of, i, :, span(part)],
+                    zl_s.at[0, part],
+                    zl_r.at[part_of, i, part],
+                    core_dev,
+                ).wait_recv()
+                total = total + ig_in[part_of, i, :, span(part)].astype(F32)
+            ig_out[pl.ds(part_of * GROUP, GROUP), span(part)] = total.astype(BF16)
 
     drain(CHUNKS - 1)
     xt_copy.wait()
@@ -450,10 +476,10 @@
             dma((STEPS,)),
             dma((3, CHUNKS, 7)),
             dma((3, CHUNKS, 7)),
-            dma((CHUNKS, 3)),
-            dma((CHUNKS, 3)),
-            dma((CHUNKS,)),
-            dma((CHUNKS // 4, 3)),
+            dma((CHUNKS, 3, PARTS)),
+            dma((CHUNKS, 3, PARTS)),
+            dma((CHUNKS, PARTS)),
+            dma((CHUNKS // 4, 3, PARTS)),
         ],
         compiler_params=pltpu.CompilerParams(
             collective_id=0, has_side_effects=True, vmem_limit_bytes=58 * 2**20

time: 83.4 us -> 82 us (0.983)
  Pallas kernels: 82.7 us -> 81.3 us
    pallas_call x1, Pallas kernels: 76.7 us -> 75.3 us  [exchange(): pl.pallas_call(exchange_kernel, out_shape=(jax.ShapeDtypeStruct((3, 4, CH...]
where the time goes in v5:
time: 82 us; the launch traced here: 81.9 us
  Pallas kernels  81.3 us (99%)
    pallas_call x1, Pallas kernels, exchange(): pl.pallas_call(exchange_kernel, out_shape=(jax.ShapeDtypeStruct((3, 4, CH...  75.3 us
    pallas_call x1, Pallas kernels, grads(): pl.pallas_call(grads_kernel, out_shape=(jax.ShapeDtypeStruct((DIM, FF), B...  6.02 us

profile of v5, /device:TPU:32, one launch (start us, length us, event | category | flops | bytes accessed | tf_op | source)
XLA Modules:
  0.0 81.9 jit_solution(10141057502904003205)
XLA Ops:
  0.6 75.3 %exchange.1 = (bf16[3,4,4,32,1792]{4,3,2,1,0:T(8,128)(2,1)}, bf16[512,512]{1,0:T(8,128)(2,1)}, bf16[32,512]{1,0:T(8,128)(2,1)}) custom-call(bf16[4,4,32,512]{3,2,1,0:T(8,128)(2,1)} %bitcast.6, bf16[4,4,32,512]{3,2,1,0:T(8,128)(2,1)} %bitcast.5, bf16[512,1792]{1,0:T(8,128)(2,1)} %wg_hbm.1, bf16[512,1792]{1,0:T(8,128)(2,1)} %wu_hbm.1, ...), custom_call_target="tpu_custom_call" | custom-call | tf_op jit(solution)/shard_map/exchange/pallas_call | solution.py:437
  75.9 6.0 %grads.1 = (bf16[512,1792]{1,0:T(8,128)(2,1)}, bf16[512,1792]{1,0:T(8,128)(2,1)}, bf16[1792,512]{1,0:T(8,128)(2,1)}, bf16[32,512]{1,0:T(8,128)(2,1)}) custom-call(bf16[512,512]{1,0:T(8,128)(2,1)} %get-tuple-element.11.xt_hbm, bf16[512,512]{1,0:T(8,128)(2,1)} %og_hbm.1, bf16[3,512,1792]{2,1,0:T(8,128)(2,1)} %bitcast.4, s32[4,14]{1,0:T(4,128)} %gm_hbm.3, ...), custom_call_target="tpu_custom_call" | custom-call | tf_op jit(solution)/shard_map/grads/pallas_call | solution.py:574

commit v6 on v5

--- a/solution.py
+++ b/solution.py
@@ -47,11 +47,11 @@
 
 def exchange_kernel(
     x_hbm, og_hbm, wg_hbm, wu_hbm, wd_hbm, gm_hbm, um_hbm, dm_hbm,
-    d_hbm, xt_hbm, ig_out,
+    h_hbm, gate_hbm, up_hbm, xt_hbm, ig_out,
     gm, um, dm, x_own, og_own, xt, w_own, wd_own, core_out, core_in,
     part, send, ring, z_out, z_in, sums, deltas,
     ig, ig_x, ig_z, ig_sum, ig_in,
-    local_sem, mask_sem, core_s, core_r, ring_s, ring_r, z_s, z_r, ag_s, ag_r, x_s, x_r, zl_s, zl_r,
+    local_sem, mask_sem, out_sem, core_s, core_r, ring_s, ring_r, z_s, z_r, ag_s, ag_r, x_s, x_r, zl_s, zl_r,
 ):
     row = lax.axis_index("row")
     col = lax.axis_index("col")
@@ -190,13 +190,9 @@
         copy(4, down, 0, right).wait_send()
         copy(5, up, 1, left).wait_send()
 
-    def out_copy(k):
-        return pltpu.make_async_copy(
-            deltas.at[pl.ds(1, 2), k], d_hbm.at[pl.ds(1, 2), :, chunk(k)], local_sem.at[7 + k]
-        )
-
-    def hidden_store(k):
-        return pltpu.make_async_copy(deltas.at[0, k], d_hbm.at[0, :, chunk(k)], local_sem.at[7 + CHUNKS + k])
+    def out_copy(m, k):
+        out = (h_hbm, gate_hbm, up_hbm)[m]
+        return pltpu.make_async_copy(deltas.at[m, k], out.at[:, chunk(k)], out_sem.at[m, k])
 
     xt_copy = pltpu.make_async_copy(xt, xt_hbm, local_sem.at[6])
 
@@ -252,8 +248,8 @@
             for part in range(PARTS):
                 zl_copy(k, part).wait_send()
 
-        out_copy(k).wait()
-        hidden_store(k).wait()
+        for m in range(3):
+            out_copy(m, k).wait()
 
     def at_chunk(s, lag, fn, count=CHUNKS):
         @pl.when((s >= lag + 2) & (s < 3 * count + lag) & (lax.rem(s + 3 * 32 - lag, 3) == 2))
@@ -393,13 +389,14 @@
                 ig[k, :, :, span(part)] = ig[k, :, :, span(part)] + value
                 for d in (2, 1, 3):
                     x_copy(k, d, part).start()
-            out_copy(k).start()
+            out_copy(1, k).start()
+            out_copy(2, k).start()
             gather_rest(y_copy(0, k))
             pair_copy(0, k, own_cols).start()
 
         def finish(k):
             pair_copy(0, k, oth_cols).wait_recv()
-            hidden_store(k).start()
+            out_copy(0, k).start()
             reduce_col(k)
 
             @pl.when(k > 0)
@@ -437,12 +434,14 @@
     return pl.pallas_call(
         exchange_kernel,
         out_shape=(
-            jax.ShapeDtypeStruct((3, 4, CHUNKS, GROUP, FF), BF16),
+            jax.ShapeDtypeStruct((4, CHUNKS, GROUP, FF), BF16),
+            jax.ShapeDtypeStruct((4, CHUNKS, GROUP, FF), BF16),
+            jax.ShapeDtypeStruct((4, CHUNKS, GROUP, FF), BF16),
             jax.ShapeDtypeStruct((DIM, TOK), BF16),
             jax.ShapeDtypeStruct((32, DIM), BF16),
         ),
         in_specs=[any_spec] * 8,
-        out_specs=(any_spec, any_spec, pl.BlockSpec(memory_space=pltpu.VMEM)),
+        out_specs=(any_spec,) * 4 + (pl.BlockSpec(memory_space=pltpu.VMEM),),
         scratch_shapes=[
             small,
             small,
@@ -466,8 +465,9 @@
             pltpu.VMEM((CHUNKS, GROUP, DIM), BF16),
             pltpu.VMEM((CHUNKS // 4, GROUP, DIM), F32),
             pltpu.VMEM((CHUNKS // 4, 3, GROUP, DIM), BF16),
-            dma((7 + 2 * CHUNKS,)),
+            dma((7,)),
             dma((3,)),
+            dma((3, CHUNKS)),
             dma((STEPS,)),
             dma((STEPS,)),
             dma((6, STEPS)),
@@ -482,7 +482,7 @@
             dma((CHUNKS // 4, 3, PARTS)),
         ],
         compiler_params=pltpu.CompilerParams(
-            collective_id=0, has_side_effects=True, vmem_limit_bytes=58 * 2**20
+            collective_id=0, has_side_effects=True, vmem_limit_bytes=46 * 2**20
         ),
         name="exchange",
     )(
@@ -498,28 +498,20 @@
 
 
 def grads_kernel(
-    xt_hbm, og_hbm, d_hbm, gm_hbm, um_hbm, dm_hbm, ig_hbm,
+    xt, og_hbm, h_in, gate_in, up_in, gm_hbm, um_hbm, dm_hbm, ig_hbm,
     gate_hbm, up_hbm, down_hbm, ig_out_hbm,
-    gm, um, dm, ig, xt, og, d, cols_out, rows_out, sem_in, sem_out,
+    gm, um, dm, ig, og, cols_out, rows_out, sem_in, sem_out,
 ):
-    head = pl.ds(0, 768)
-    tail = pl.ds(768, FF - 768)
     loads = [
-        pltpu.make_async_copy(xt_hbm, xt, sem_in.at[0]),
-        pltpu.make_async_copy(d_hbm.at[1, :, head], d.at[1, :, head], sem_in.at[1]),
-        pltpu.make_async_copy(gm_hbm, gm, sem_in.at[2]),
-        pltpu.make_async_copy(d_hbm.at[1, :, tail], d.at[1, :, tail], sem_in.at[3]),
-        pltpu.make_async_copy(um_hbm, um, sem_in.at[4]),
-        pltpu.make_async_copy(d_hbm.at[2], d.at[2], sem_in.at[5]),
-        pltpu.make_async_copy(dm_hbm, dm, sem_in.at[6]),
-        pltpu.make_async_copy(ig_hbm, ig, sem_in.at[7]),
-        pltpu.make_async_copy(og_hbm, og, sem_in.at[8]),
-        pltpu.make_async_copy(d_hbm.at[0], d.at[0], sem_in.at[9]),
+        pltpu.make_async_copy(gm_hbm, gm, sem_in.at[0]),
+        pltpu.make_async_copy(um_hbm, um, sem_in.at[1]),
+        pltpu.make_async_copy(dm_hbm, dm, sem_in.at[2]),
+        pltpu.make_async_copy(ig_hbm, ig, sem_in.at[3]),
+        pltpu.make_async_copy(og_hbm, og, sem_in.at[4]),
     ]
     for load in loads:
         load.start()
-    for load in loads[:3]:
-        load.wait()
+    loads[0].wait()
     ig_store = pltpu.make_async_copy(ig, ig_out_hbm, sem_out.at[2 + FF // 256])
     stores = [
         pltpu.make_async_copy(cols_out.at[0], gate_hbm, sem_out.at[0]),
@@ -527,12 +519,10 @@
     ]
     for which, mask in ((1, gm), (2, um)):
         if which == 2:
-            loads[4].wait()
-            loads[5].wait()
+            loads[1].wait()
+        source = (gate_in, up_in)[which - 1]
         for j in range(FF // 256):
-            if which == 1 and j == 3:
-                loads[3].wait()
-            value = product(xt[...], d[which, :, j * 256 : (j + 1) * 256])
+            value = product(xt[...], source[:, j * 256 : (j + 1) * 256])
             for k in range(2):
                 cols = pl.ds(j * 256 + k * BLOCK, BLOCK)
                 for i in range(DIM // BLOCK):
@@ -542,7 +532,7 @@
                     cols_out[which - 1, rows, cols] = part.astype(BF16)
 
         stores[which - 1].start()
-    for load in loads[6:]:
+    for load in loads[2:]:
         load.wait()
     ig_store.start()
 
@@ -551,7 +541,7 @@
         return pltpu.make_async_copy(rows_out.at[rows], down_hbm.at[rows], sem_out.at[2 + j])
 
     for j in range(FF // 256):
-        value = t_product(d[0, :, j * 256 : (j + 1) * 256], og[...])
+        value = t_product(h_in[:, j * 256 : (j + 1) * 256], og[...])
         for k in range(2):
             rows = pl.ds(j * 256 + k * BLOCK, BLOCK)
             for i in range(DIM // BLOCK):
@@ -568,8 +558,9 @@
         store_rows(j).wait()
 
 
-def grads(turned, out_grad, deltas, gate_mask, up_mask, down_mask, ig):
+def grads(turned, out_grad, hidden, gate, up, gate_mask, up_mask, down_mask, ig):
     any_spec = pl.BlockSpec(memory_space=pl.ANY)
+    vmem = pl.BlockSpec(memory_space=pltpu.VMEM)
     small = pltpu.SMEM((DIM // BLOCK, FF // BLOCK), jnp.int32)
     return pl.pallas_call(
         grads_kernel,
@@ -579,30 +570,28 @@
             jax.ShapeDtypeStruct((FF, DIM), BF16),
             jax.ShapeDtypeStruct((32, DIM), BF16),
         ),
-        in_specs=[any_spec] * 7,
+        in_specs=[vmem, any_spec, vmem, vmem, vmem] + [any_spec] * 4,
         out_specs=(any_spec,) * 4,
         scratch_shapes=[
             small,
             small,
             small,
             pltpu.VMEM((32, DIM), BF16),
-            pltpu.VMEM((DIM, TOK), BF16),
             pltpu.VMEM((TOK, DIM), BF16),
-            pltpu.VMEM((3, TOK, FF), BF16),
             pltpu.VMEM((2, DIM, FF), BF16),
             pltpu.VMEM((FF, DIM), BF16),
-            pltpu.SemaphoreType.DMA((10,)),
+            pltpu.SemaphoreType.DMA((5,)),
             pltpu.SemaphoreType.DMA((3 + FF // 256,)),
         ],
-        compiler_params=pltpu.CompilerParams(vmem_limit_bytes=62 * 2**20),
+        compiler_params=pltpu.CompilerParams(vmem_limit_bytes=44 * 2**20),
         name="grads",
-    )(turned, out_grad, deltas, gate_mask, up_mask, down_mask.T, ig)
+    )(turned, out_grad, hidden, gate, up, gate_mask, up_mask, down_mask.T, ig)
 
 
 def shards(inputs, out_grad, gate_weight, up_weight, down_weight, gate_mask, up_mask, down_mask):
-    deltas, turned, ig = exchange(inputs, out_grad, gate_weight, up_weight, down_weight, gate_mask, up_mask, down_mask)
-    deltas = deltas.reshape(3, TOK, FF)
-    gate_grad, up_grad, down_grad, input_grad = grads(turned, out_grad, deltas, gate_mask, up_mask, down_mask, ig)
+    hidden, gate, up, turned, ig = exchange(inputs, out_grad, gate_weight, up_weight, down_weight, gate_mask, up_mask, down_mask)
+    hidden, gate, up = (value.reshape(TOK, FF) for value in (hidden, gate, up))
+    gate_grad, up_grad, down_grad, input_grad = grads(turned, out_grad, hidden, gate, up, gate_mask, up_mask, down_mask, ig)
     return (input_grad, gate_grad, up_grad, down_grad)
 
 

time: 82 us -> 84.6 us (1.032)
  local copies, waits for them, and re-layouts: 0 us -> 4.12 us
  Pallas kernels: 81.3 us -> 79.6 us
    unnamed x0 -> x12, local copies, waits for them, and re-layouts: none -> 4.12 us
    pallas_call x1, Pallas kernels: 6.02 us -> 5.07 us  [grads(): pl.pallas_call(grads_kernel, out_shape=(jax.ShapeDtypeStruct((DIM, FF), B...]
where the time goes in v6:
time: 84.6 us; the launch traced here: 84.3 us
  Pallas kernels  79.6 us (94%)
  local copies, waits for them, and re-layouts  4.12 us (5%)
    pallas_call x1, Pallas kernels, exchange(): pl.pallas_call(exchange_kernel, out_shape=(jax.ShapeDtypeStruct((4, CHUNK...  74.5 us
    pallas_call x1, Pallas kernels, grads(): pl.pallas_call(grads_kernel, out_shape=(jax.ShapeDtypeStruct((DIM, FF), B...  5.07 us
    unnamed x12, local copies, waits for them, and re-layouts  4.12 us

profile of v6, /device:TPU:32, one launch (start us, length us, event | category | flops | bytes accessed | tf_op | source)
XLA Modules:
  0.0 84.3 jit_solution(10537052052905908275)
XLA Ops:
  0.6 0.0 copy-start
  0.6 1.0 %copy-done = bf16[512,512]{1,0:T(8,128)(2,1)S(1)} copy-done((bf16[512,512]{1,0:T(8,128)(2,1)S(1)}, bf16[512,512]{1,0:T(8,128)(2,1)}, u32[]{:S(2)}) %copy-start) | copy-done | bytes 524312
  1.7 0.0 copy-start.2
  1.7 1.0 %copy-done.2 = bf16[512,512]{1,0:T(8,128)(2,1)S(1)} copy-done((bf16[512,512]{1,0:T(8,128)(2,1)S(1)}, bf16[512,512]{1,0:T(8,128)(2,1)}, u32[]{:S(2)}) %copy-start.2) | copy-done | bytes 524312
  2.7 0.0 copy-start.3
  2.7 0.7 copy-done.3
  3.4 0.0 copy-start.4
  3.4 0.7 copy-done.4
  4.1 0.0 copy-start.5
  4.1 0.7 copy-done.5
  4.8 0.0 copy-start.1
  4.8 74.5 %exchange.1 = (bf16[4,4,32,1792]{3,2,1,0:T(8,128)(2,1)S(1)}, bf16[4,4,32,1792]{3,2,1,0:T(8,128)(2,1)S(1)}, bf16[4,4,32,1792]{3,2,1,0:T(8,128)(2,1)S(1)}, bf16[512,512]{1,0:T(8,128)(2,1)S(1)}, bf16[32,512]{1,0:T(8,128)(2,1)S(1)}) custom-call(bf16[4,4,32,512]{3,2,1,0:T(8,128)(2,1)S(1)} %bitcast.10, bf16[4,4,32,512]{3,2,1,0:T(8,128)(2,1)S(1)} %bitcast.6, ...), custom_call_target="tpu_custom_call" | custom-call | tf_op jit(solution)/shard_map/exchange/pallas_call | solution.py:434
  79.3 0.0 copy-done.1
  79.3 5.1 %grads.1 = (bf16[512,1792]{1,0:T(8,128)(2,1)}, bf16[512,1792]{1,0:T(8,128)(2,1)}, bf16[1792,512]{1,0:T(8,128)(2,1)}, bf16[32,512]{1,0:T(8,128)(2,1)}) custom-call(bf16[512,512]{1,0:T(8,128)(2,1)S(1)} %get-tuple-element.13.xt, bf16[512,512]{1,0:T(8,128)(2,1)S(1)} %copy-done.1, bf16[512,1792]{1,0:T(8,128)(2,1)S(1)} %bitcast.7, bf16[512,1792]{1,0:T(8,128)(2,1)S(1)} %bitcast.8, ...), custom_call_target="tpu_custom_call" | custom-call | tf_op jit(solution)/shard_map/grads/pallas_call | solution.py:565
Async XLA Ops:
  0.6 1.0 %copy-start = (bf16[512,512]{1,0:T(8,128)(2,1)S(1)}, bf16[512,512]{1,0:T(8,128)(2,1)}, u32[]{:S(2)}) copy-start(bf16[512,512]{1,0:T(8,128)(2,1)} %og_hbm.1) | copy-start | bytes 1572868
  1.7 1.0 %copy-start.2 = (bf16[512,512]{1,0:T(8,128)(2,1)S(1)}, bf16[512,512]{1,0:T(8,128)(2,1)}, u32[]{:S(2)}) copy-start(bf16[512,512]{1,0:T(8,128)(2,1)} %param.8) | copy-start | bytes 1572868
  2.7 0.7 copy-start.3
  3.4 0.7 copy-start.4
  4.1 0.7 copy-start.5
  4.8 74.5 %copy-start.1 = (bf16[512,512]{1,0:T(8,128)(2,1)S(1)}, bf16[512,512]{1,0:T(8,128)(2,1)}, u32[]{:S(2)}) copy-start(bf16[512,512]{1,0:T(8,128)(2,1)} %og_hbm.1) | copy-start | bytes 1572868
